TPU v7x, 512 devices: a whole 4x8x8 slice. The times are simulated.
512 devices in a mesh: bx: 16 (over x, z_hi), by: 4 (over z_lo, core), bz: 8 (over y).
Axes of the slice: x: 4, y: 8, z: 8 (z_hi: 4, z_lo: 2; z = z_hi * 2 + z_lo), core: 2. Of those that a mesh axis runs over, the one named last changes fastest.
Arguments:
- forcing: float32 [256, 256, 512], P('bx', 'bz', 'by'), may hold values from -6 to 6
- start: float32 [256, 256, 512], P('bx', 'bz', 'by'), may hold values from -2 to 2
- element_class_index: int32 [64, 64, 128], P('bx', 'bz', 'by'), may hold values from 0 to 15
- class_coef: float32 [3, 16], replicated, may hold values from 0.3 to 3
Outputs:
- solution: float32 [256, 256, 512], P('bx', 'bz', 'by')
- residual: float32 [256, 256, 512], P('bx', 'bz', 'by')
All inputs are finite; a program needn't handle non-finite values.
Results may differ from a plain program's by a relative error of at most 0.015.
Values may be sent and summed in bfloat16 or wider, within the bound.
A program may use at most 64 MiB of HBM per device.

v0:
```python
import math

import jax
import jax.numpy as jnp
from jax import lax
from jax.sharding import PartitionSpec as P

CYCLES = 2


FACE_PENALTY = 2.0
DAMPING = 0.6666666666666666


def extended(value, sides, width):
    for axis, dim in sides:
        devices, length = (lax.axis_size(axis), value.shape[dim])
        up = [(i, (i + 1) % devices) for i in range(devices - 1)]
        down = [(j, i) for i, j in up]
        last = lax.slice_in_dim(value, length - width, length, axis=dim)
        first = lax.slice_in_dim(value, 0, width, axis=dim)
        before = lax.ppermute(last, axis, up)
        after = lax.ppermute(first, axis, down)
        value = jnp.concatenate([before, value, after], axis=dim)
    return value


def face_factor(count):
    edges = jnp.arange(count + 1, dtype=jnp.int32)
    return jnp.where(edges % 4 == 0, FACE_PENALTY, 1.0).astype(jnp.float32)


def edge_weights(kappa_pad):
    inner_x = kappa_pad[:, 1:-1, 1:-1]
    weight_x = face_factor(inner_x.shape[0] - 2)[:, None, None] * (
        (inner_x[:-1] + inner_x[1:]) * 0.5
    )
    inner_z = kappa_pad[1:-1, :, 1:-1]
    weight_z = face_factor(inner_z.shape[1] - 2)[None, :, None] * (
        (inner_z[:, :-1] + inner_z[:, 1:]) * 0.5
    )
    inner_y = kappa_pad[1:-1, 1:-1, :]
    quadrature_weight_y = face_factor(inner_y.shape[2] - 2)[None, None, :] * (
        (inner_y[:, :, :-1] + inner_y[:, :, 1:]) * 0.5
    )
    return (weight_x, weight_z, quadrature_weight_y)


def operator_diagonal(weights, sigma_node):
    weight_x, weight_z, quadrature_weight_y = weights
    total = sigma_node + (weight_x[:-1] + weight_x[1:])
    total = total + (weight_z[:, :-1] + weight_z[:, 1:])
    return total + (quadrature_weight_y[:, :, :-1] + quadrature_weight_y[:, :, 1:])


def apply_operator(field_pad, weights, sigma_node):
    weight_x, weight_z, quadrature_weight_y = weights
    centre = field_pad[1:-1, 1:-1, 1:-1]
    total = sigma_node * centre
    total = (
        total
        + weight_x[:-1] * (centre - field_pad[:-2, 1:-1, 1:-1])
        + weight_x[1:] * (centre - field_pad[2:, 1:-1, 1:-1])
    )
    total = (
        total
        + weight_z[:, :-1] * (centre - field_pad[1:-1, :-2, 1:-1])
        + weight_z[:, 1:] * (centre - field_pad[1:-1, 2:, 1:-1])
    )
    total = (
        total
        + quadrature_weight_y[:, :, :-1] * (centre - field_pad[1:-1, 1:-1, :-2])
        + quadrature_weight_y[:, :, 1:] * (centre - field_pad[1:-1, 1:-1, 2:])
    )
    return total


def padded_field(field):
    return extended(field, (("bx", 0), ("bz", 1), ("by", 2)), 1)


def node_field(element_values):
    return jnp.repeat(jnp.repeat(jnp.repeat(element_values, 4, 0), 4, 1), 4, 2)


def restrict_matrix():
    return (
        jnp.array(
            [[1.0, 2.0 / 3.0, 1.0 / 3.0, 0.0], [0.0, 1.0 / 3.0, 2.0 / 3.0, 1.0]], dtype=jnp.float32
        )
        * 0.5
    )


def prolong_matrix():
    return jnp.array(
        [[1.0, 0.0], [2.0 / 3.0, 1.0 / 3.0], [1.0 / 3.0, 2.0 / 3.0], [0.0, 1.0]], dtype=jnp.float32
    )


def restrict_field(field):
    count_x, count_z, count_y = (field.shape[0] // 4, field.shape[1] // 4, field.shape[2] // 4)
    blocks = field.reshape(count_x, 4, count_z, 4, count_y, 4)
    matrix = restrict_matrix()
    blocks = jnp.einsum("ai,pizjyk->pazjyk", matrix, blocks, precision=lax.Precision.HIGHEST)
    blocks = jnp.einsum("bj,pazjyk->pazbyk", matrix, blocks, precision=lax.Precision.HIGHEST)
    blocks = jnp.einsum("ck,pazbyk->pazbyc", matrix, blocks, precision=lax.Precision.HIGHEST)
    return blocks.reshape(2 * count_x, 2 * count_z, 2 * count_y)


def prolong_field(coarse):
    count_x, count_z, count_y = (coarse.shape[0] // 2, coarse.shape[1] // 2, coarse.shape[2] // 2)
    blocks = coarse.astype(jnp.float32).reshape(count_x, 2, count_z, 2, count_y, 2)
    matrix = prolong_matrix()
    blocks = jnp.einsum("ia,pazbyc->pizbyc", matrix, blocks, precision=lax.Precision.HIGHEST)
    blocks = jnp.einsum("jb,pizbyc->pizjyc", matrix, blocks, precision=lax.Precision.HIGHEST)
    blocks = jnp.einsum("kc,pizjyc->pizjyk", matrix, blocks, precision=lax.Precision.HIGHEST)
    return blocks.reshape(4 * count_x, 4 * count_z, 4 * count_y)


def sine_rows(index_zero, count):
    index_one = index_zero + 1
    product = (index_one[:, None] * index_one[None, :]).astype(jnp.float32)
    return (jnp.sin(product * (math.pi / (count + 1))) * math.sqrt(2.0 / (count + 1))).astype(
        jnp.bfloat16
    )


def spectrum_values(index_zero, count):
    return 2.0 - 2.0 * jnp.cos((index_zero + 1).astype(jnp.float32) * (math.pi / (count + 1)))


def class_values(element_class_index, class_coef):
    labels = jnp.arange(class_coef.shape[1], dtype=jnp.int32)
    onehot = (element_class_index[..., None] == labels).astype(jnp.float32)
    return tuple((jnp.sum(onehot * class_coef[row], axis=-1) for row in range(3)))


def coarse_correction(resid, kappa_mean, sigma_mean):
    count_bx, count_by, count_bz = (lax.axis_size("bx"), lax.axis_size("by"), lax.axis_size("bz"))
    coarse = restrict_field(resid).astype(jnp.bfloat16)
    pencil = lax.all_to_all(coarse, "by", split_axis=0, concat_axis=2, tiled=True)
    count_y = pencil.shape[2]
    table_y = sine_rows(jnp.arange(count_y, dtype=jnp.int32), count_y)
    pencil = jnp.dot(pencil, table_y, preferred_element_type=jnp.float32).astype(jnp.bfloat16)
    pencil = lax.all_to_all(pencil, "bz", split_axis=2, concat_axis=1, tiled=True)
    count_z = pencil.shape[1]
    table_z = sine_rows(jnp.arange(count_z, dtype=jnp.int32), count_z)
    pencil = jnp.einsum("ab,xbc->xac", table_z, pencil, preferred_element_type=jnp.float32).astype(
        jnp.bfloat16
    )
    pencil = lax.all_to_all(pencil, ("bx", "by"), split_axis=1, concat_axis=0, tiled=True)
    count_x = pencil.shape[0]
    x_index = jnp.arange(count_x, dtype=jnp.int32)
    table_x = sine_rows(x_index, count_x)
    local_z = pencil.shape[1]
    local_y = pencil.shape[2]
    z_index = (lax.axis_index("bx") * count_by + lax.axis_index("by")) * local_z + jnp.arange(
        local_z, dtype=jnp.int32
    )
    y_index = lax.axis_index("bz") * local_y + jnp.arange(local_y, dtype=jnp.int32)
    eigen_x = spectrum_values(x_index, count_x)
    eigen_z = spectrum_values(z_index, local_z * count_bx * count_by)
    eigen_y = spectrum_values(y_index, local_y * count_bz)
    eigen_sum = (
        kappa_mean * (eigen_x[:, None, None] + eigen_z[None, :, None] + eigen_y[None, None, :])
        + sigma_mean
    )
    pencil = (
        jnp.einsum("ab,bzy->azy", table_x, pencil, preferred_element_type=jnp.float32) / eigen_sum
    ).astype(jnp.bfloat16)
    pencil = jnp.einsum("ab,bzy->azy", table_x, pencil, preferred_element_type=jnp.float32).astype(
        jnp.bfloat16
    )
    pencil = lax.all_to_all(pencil, ("bx", "by"), split_axis=0, concat_axis=1, tiled=True)
    pencil = jnp.einsum("ab,xbc->xac", table_z, pencil, preferred_element_type=jnp.float32).astype(
        jnp.bfloat16
    )
    pencil = lax.all_to_all(pencil, "bz", split_axis=1, concat_axis=2, tiled=True)
    pencil = jnp.dot(pencil, table_y, preferred_element_type=jnp.float32).astype(jnp.bfloat16)
    coarse = lax.all_to_all(pencil, "by", split_axis=2, concat_axis=0, tiled=True)
    return prolong_field(coarse)


def body(forcing, start, element_class_index, class_coef):
    kappa_elem, sigma_elem, beta_elem = class_values(element_class_index, class_coef)
    kappa_node = node_field(kappa_elem)
    sigma_node = node_field(sigma_elem)
    beta_node = node_field(beta_elem)
    kappa_pad = extended(kappa_node, (("bx", 0), ("bz", 1), ("by", 2)), 1)
    weights = edge_weights(kappa_pad)
    diagonal = operator_diagonal(weights, sigma_node)
    kappa_mean = jnp.mean(class_coef[0])
    sigma_mean = jnp.mean(class_coef[1])

    def nonlinear_residual(solution):
        return (
            forcing
            - apply_operator(padded_field(solution), weights, sigma_node)
            - beta_node * solution * solution * solution
        )

    solution = start
    for iteration in range(CYCLES):
        resid = nonlinear_residual(solution)
        smooth_one = DAMPING * resid / diagonal
        smooth_two = (
            smooth_one
            + DAMPING
            * (resid - apply_operator(padded_field(smooth_one), weights, sigma_node))
            / diagonal
        )
        solution = solution + smooth_two + coarse_correction(resid, kappa_mean, sigma_mean)
    return (solution, nonlinear_residual(solution))


def solution(mesh):
    in_specs = (P("bx", "bz", "by"), P("bx", "bz", "by"), P("bx", "bz", "by"), P())
    out_specs = (P("bx", "bz", "by"), P("bx", "bz", "by"))
    return jax.shard_map(body, mesh=mesh, in_specs=in_specs, out_specs=out_specs, check_vma=False)
```

profile of v0, /device:TPU:78, one launch (start us, length us, event | category | flops | bytes accessed | tf_op | source)
XLA Modules:
  0.0 406.9 jit_solution(6416141053726972275)
XLA Ops:
  3.3 10.3 %collective-permute-start.1 = (f32[1,32,128]{2,1,0:T(8,128)S(1)}, f32[1,32,128]{2,1,0:T(8,128)S(1)}, u32[]{:S(2)}, u32[]{:S(2)}) collective-permute-start(f32[1,32,128]{2,1,0:T(8,128)S(1)} %copy.418), channel_id=1, source_target_pairs={{32,0},{64,32},{96,64},{128,96},{160,128},{192,160},{224,192},{256... | collective-permute-start | bytes 49160 | tf_op jit(solution)/shard_map/ppermute | solution.py:23
  16.5 2.2 collective-permute-start.2
  18.7 6.7 %collective-permute-start.3 = (f32[1,32,128]{2,1,0:T(8,128)S(1)}, f32[1,32,128]{2,1,0:T(8,128)S(1)}, u32[]{:S(2)}, u32[]{:S(2)}) collective-permute-start(f32[1,32,128]{2,1,0:T(8,128)S(1)} %get-tuple-element.52), channel_id=1, source_target_pairs={{32,0},{64,32},{96,64},{128,96},{160,128},{192,160},{224,192},{256... | collective-permute-start | bytes 49160 | tf_op jit(solution)/shard_map/ppermute | solution.py:23
  29.0 2.4 collective-permute-start.5
  31.3 3.5 collective-permute-start.4
  34.9 2.4 collective-permute-start.7
  37.3 3.5 collective-permute-start.6
  43.1 2.4 collective-permute-start.8
  45.7 3.1 collective-permute-start.11
  48.9 2.1 collective-permute-start.10
  53.9 3.8 collective-permute-done.10
  58.9 10.1 %reshape.196 = f32[4,4,8,4,32,4]{5,4,3,2,1,0:T(8,128)} reshape(f32[16,32,128]{2,1,0:T(8,128)S(1)} %get-tuple-element.19) | data formatting | bytes 524288 | tf_op jit(solution)/shard_map/reshape | solution.py:103
  69.0 5.9 %copy.426 = f32[4,4,8,4,32,4]{4,1,5,3,2,0:T(4,128)S(1)} copy(f32[4,4,8,4,32,4]{5,4,3,2,1,0:T(8,128)} %reshape.196) | data formatting | bytes 524288 | tf_op jit(solution)/shard_map/reshape | solution.py:103
  82.6 3.3 all-to-all-start
  90.7 7.7 %all-to-all-start.1 = ((bf16[8,2,512]{2,1,0:T(2,128)(2,1)}), bf16[8,2,512]{2,1,0:T(2,128)(2,1)S(1)}, u32[]{:S(2)}, u32[]{:S(2)}) async-start(bf16[8,2,512]{2,1,0:T(2,128)(2,1)} %reshape.216), calls=%async_computation.1 | async-start | bytes 32768 | tf_op jit(solution)/shard_map/all_to_all | solution.py:146
  99.8 5.0 %all-to-all-done.1 = bf16[8,2,512]{2,1,0:T(2,128)(2,1)S(1)} async-done(((bf16[8,2,512]{2,1,0:T(2,128)(2,1)}), bf16[8,2,512]{2,1,0:T(2,128)(2,1)S(1)}, u32[]{:S(2)}, u32[]{:S(2)}) %all-to-all-start.1) | async-done | bytes 16416 | tf_op jit(solution)/shard_map/all_to_all | solution.py:146
  106.2 9.1 %all-to-all-start.2 = ((bf16[2,128,32]{2,0,1:T(2,128)(2,1)}), bf16[2,128,32]{2,0,1:T(2,128)(2,1)S(1)}, u32[]{:S(2)}, u32[]{:S(2)}) async-start(bf16[2,128,32]{2,0,1:T(2,128)(2,1)} %copy.434), calls=%async_computation.2 | async-start | bytes 131072 | tf_op jit(solution)/shard_map/all_to_all | solution.py:152
  115.4 4.8 %collective-permute-start.13 = (f32[1,32,128]{2,1,0:T(8,128)S(1)}, f32[1,32,128]{2,1,0:T(8,128)S(1)}, u32[]{:S(2)}, u32[]{:S(2)}) collective-permute-start(f32[1,32,128]{2,1,0:T(8,128)S(1)} %get-tuple-element.51), channel_id=1, source_target_pairs={{32,0},{64,32},{96,64},{128,96},{160,128},{192,160},{224,192},{256... | collective-permute-start | bytes 49160 | tf_op jit(solution)/shard_map/ppermute | solution.py:23
  120.2 2.3 collective-permute-start.12
  125.1 10.6 %all-to-all-start.3 = ((bf16[128,2,32]{2,1,0:T(2,128)(2,1)}), bf16[128,2,32]{2,1,0:T(2,128)(2,1)S(1)}, u32[]{:S(2)}, u32[]{:S(2)}) async-start(bf16[128,2,32]{2,1,0:T(2,128)(2,1)} %copy.438), calls=%async_computation.3 | async-start | bytes 131072 | tf_op jit(solution)/shard_map/all_to_all | solution.py:175
  135.8 3.3 collective-permute-start.15
  139.1 2.5 collective-permute-start.14
  144.2 4.7 %all-to-all-start.4 = ((bf16[8,2,512]{2,1,0:T(2,128)(2,1)}), bf16[8,2,512]{2,1,0:T(2,128)(2,1)S(1)}, u32[]{:S(2)}, u32[]{:S(2)}) async-start(bf16[8,2,512]{2,1,0:T(2,128)(2,1)} %reshape.218), calls=%async_computation.4 | async-start | bytes 32768 | tf_op jit(solution)/shard_map/all_to_all | solution.py:179
  148.9 6.3 %all-to-all-done.4 = bf16[8,2,512]{2,1,0:T(2,128)(2,1)S(1)} async-done(((bf16[8,2,512]{2,1,0:T(2,128)(2,1)}), bf16[8,2,512]{2,1,0:T(2,128)(2,1)S(1)}, u32[]{:S(2)}, u32[]{:S(2)}) %all-to-all-start.4) | async-done | bytes 16416 | tf_op jit(solution)/shard_map/all_to_all | solution.py:179
  158.2 4.5 %all-to-all-start.5 = ((bf16[4,2,1024]{2,1,0:T(2,128)(2,1)}), bf16[4,2,1024]{2,1,0:T(2,128)(2,1)S(1)}, u32[]{:S(2)}, u32[]{:S(2)}) async-start(bf16[4,2,1024]{2,1,0:T(2,128)(2,1)} %reshape.220), calls=%async_computation.5 | async-start | bytes 32768 | tf_op jit(solution)/shard_map/all_to_all | solution.py:181
  163.7 2.0 collective-permute-start.17
  165.7 3.0 collective-permute-start.16
  172.2 15.5 %fusion.9 = f32[4,4,8,4,32,4]{5,4,3,2,1,0:T(8,128)} fusion(f32[4,2,1,1,1,1]{0,1,5,4,3,2:T(2,128)S(1)} %copy-done.13, f32[4,4,8,4,32,2]{4,3,5,2,1,0:T(4,128)S(1)} %convolution_bitcast_fusion.2), kind=kOutput, calls=%fused_computation.37 | convolution fusion | flops 1572864 | bytes 393248 | tf_op jit(solution)/shard_map/kc,pizjyc->pizjyk/dot_general | solution.py:117
  187.7 8.2 %reshape.198 = f32[16,32,128]{2,1,0:T(8,128)S(1)} reshape(f32[4,4,8,4,32,4]{5,4,3,2,1,0:T(8,128)} %fusion.9) | data formatting | bytes 524288 | tf_op jit(solution)/shard_map/reshape | solution.py:118
  197.6 3.9 collective-permute-start.19
  201.5 2.8 collective-permute-start.18
  204.3 5.8 %collective-permute-done.18 = f32[1,32,128]{2,1,0:T(8,128)S(1)} collective-permute-done((f32[1,32,128]{2,1,0:T(8,128)S(1)}, f32[1,32,128]{2,1,0:T(8,128)S(1)}, u32[]{:S(2)}, u32[]{:S(2)}) %collective-permute-start.18) | collective-permute-done | bytes 16416 | tf_op jit(solution)/shard_map/ppermute | solution.py:22
  210.1 3.3 collective-permute-start.21
  213.5 2.7 collective-permute-start.20
  216.2 2.8 collective-permute-done.20
  221.2 2.4 collective-permute-start.22
  223.6 2.6 collective-permute-done.23
  226.2 3.8 collective-permute-done.22
  232.1 10.1 %reshape.199 = f32[4,4,8,4,32,4]{5,4,3,2,1,0:T(8,128)} reshape(f32[16,32,128]{2,1,0:T(8,128)S(1)} %get-tuple-element.16) | data formatting | bytes 524288 | tf_op jit(solution)/shard_map/reshape | solution.py:103
  242.2 5.9 %copy.454 = f32[4,4,8,4,32,4]{4,1,5,3,2,0:T(4,128)S(1)} copy(f32[4,4,8,4,32,4]{5,4,3,2,1,0:T(8,128)} %reshape.199) | data formatting | bytes 524288 | tf_op jit(solution)/shard_map/reshape | solution.py:103
  256.0 4.9 %all_to_all.210 = bf16[4,2,1024]{2,1,0:T(2,128)(2,1)S(1)} all-to-all(bf16[4,2,1024]{2,1,0:T(2,128)(2,1)S(1)} %reshape.222), channel_id=1, replica_groups=mesh['bx'=16,'by'=4,'bz'=8] {'by'}, dimensions={0} | all-to-all | bytes 32768 | tf_op jit(solution)/shard_map/all_to_all | solution.py:142
  263.3 12.0 %all_to_all.211 = bf16[8,2,512]{2,1,0:T(2,128)(2,1)S(1)} all-to-all(bf16[8,2,512]{2,1,0:T(2,128)(2,1)S(1)} %reshape.224), channel_id=1, replica_groups=mesh['bx'=16,'by'=4,'bz'=8] {'bz'}, dimensions={0} | all-to-all | bytes 32768 | tf_op jit(solution)/shard_map/all_to_all | solution.py:146
  277.4 8.2 %all-to-all-start.8 = ((bf16[2,128,32]{2,0,1:T(2,128)(2,1)}), bf16[2,128,32]{2,0,1:T(2,128)(2,1)S(1)}, u32[]{:S(2)}, u32[]{:S(2)}) async-start(bf16[2,128,32]{2,0,1:T(2,128)(2,1)} %copy.462), calls=%async_computation.8 | async-start | bytes 131072 | tf_op jit(solution)/shard_map/all_to_all | solution.py:152
  285.5 4.8 %collective-permute-start.25 = (f32[1,32,128]{2,1,0:T(8,128)S(1)}, f32[1,32,128]{2,1,0:T(8,128)S(1)}, u32[]{:S(2)}, u32[]{:S(2)}) collective-permute-start(f32[1,32,128]{2,1,0:T(8,128)S(1)} %get-tuple-element.47), channel_id=1, source_target_pairs={{32,0},{64,32},{96,64},{128,96},{160,128},{192,160},{224,192},{256... | collective-permute-start | bytes 49160 | tf_op jit(solution)/shard_map/ppermute | solution.py:23
  296.5 10.4 %all-to-all-start.9 = ((bf16[128,2,32]{2,1,0:T(2,128)(2,1)}), bf16[128,2,32]{2,1,0:T(2,128)(2,1)S(1)}, u32[]{:S(2)}, u32[]{:S(2)}) async-start(bf16[128,2,32]{2,1,0:T(2,128)(2,1)} %copy.466), calls=%async_computation.9 | async-start | bytes 131072 | tf_op jit(solution)/shard_map/all_to_all | solution.py:175
  306.9 3.3 collective-permute-start.27
  310.3 2.5 collective-permute-start.26
  316.0 4.7 %all-to-all-start.10 = ((bf16[8,2,512]{2,1,0:T(2,128)(2,1)}), bf16[8,2,512]{2,1,0:T(2,128)(2,1)S(1)}, u32[]{:S(2)}, u32[]{:S(2)}) async-start(bf16[8,2,512]{2,1,0:T(2,128)(2,1)} %reshape.226), calls=%async_computation.10 | async-start | bytes 32768 | tf_op jit(solution)/shard_map/all_to_all | solution.py:179
  321.3 5.8 %all-to-all-done.10 = bf16[8,2,512]{2,1,0:T(2,128)(2,1)S(1)} async-done(((bf16[8,2,512]{2,1,0:T(2,128)(2,1)}), bf16[8,2,512]{2,1,0:T(2,128)(2,1)S(1)}, u32[]{:S(2)}, u32[]{:S(2)}) %all-to-all-start.10) | async-done | bytes 16416 | tf_op jit(solution)/shard_map/all_to_all | solution.py:179
  330.0 4.5 %all-to-all-start.11 = ((bf16[4,2,1024]{2,1,0:T(2,128)(2,1)}), bf16[4,2,1024]{2,1,0:T(2,128)(2,1)S(1)}, u32[]{:S(2)}, u32[]{:S(2)}) async-start(bf16[4,2,1024]{2,1,0:T(2,128)(2,1)} %reshape.228), calls=%async_computation.11 | async-start | bytes 32768 | tf_op jit(solution)/shard_map/all_to_all | solution.py:181
  335.5 2.0 collective-permute-start.29
  337.5 3.3 collective-permute-start.28
  345.6 16.2 %fusion.6 = f32[4,4,8,4,32,4]{5,4,3,2,1,0:T(8,128)} fusion(f32[4,2,1,1,1,1]{0,1,5,4,3,2:T(2,128)} %constant.103, f32[4,4,8,4,32,2]{4,3,5,2,1,0:T(4,128)S(1)} %convolution_bitcast_fusion), kind=kOutput, calls=%fused_computation.34 | convolution fusion | flops 1572864 | bytes 393248 | tf_op jit(solution)/shard_map/kc,pizjyc->pizjyk/dot_general | solution.py:117
  361.9 8.8 %reshape.201 = f32[16,32,128]{2,1,0:T(8,128)} reshape(f32[4,4,8,4,32,4]{5,4,3,2,1,0:T(8,128)} %fusion.6) | data formatting | bytes 524288 | tf_op jit(solution)/shard_map/reshape | solution.py:118
  370.7 2.3 fusion.45
  373.1 3.9 collective-permute-start.31
  377.0 2.9 collective-permute-start.30
  379.9 5.8 %collective-permute-done.30 = f32[1,32,128]{2,1,0:T(8,128)S(1)} collective-permute-done((f32[1,32,128]{2,1,0:T(8,128)S(1)}, f32[1,32,128]{2,1,0:T(8,128)S(1)}, u32[]{:S(2)}, u32[]{:S(2)}) %collective-permute-start.30) | collective-permute-done | bytes 16416 | tf_op jit(solution)/shard_map/ppermute | solution.py:22
  385.7 3.3 collective-permute-start.33
  389.0 2.5 collective-permute-start.32
  391.5 3.0 collective-permute-done.32
  396.7 2.4 collective-permute-start.34
  399.1 2.6 collective-permute-done.35
  401.7 3.8 collective-permute-done.34
  (232 shorter events, 82.2 us)
Async XLA Ops:
  0.6 34.2 %copy-start.1 = (f32[16,32,128]{2,1,0:T(8,128)S(1)}, f32[16,32,128]{2,1,0:T(8,128)}, u32[]{:S(2)}) copy-start(f32[16,32,128]{2,1,0:T(8,128)} %param.9) | copy-start | bytes 786436
  3.3 25.6 %collective-permute-start.1 = (f32[1,32,128]{2,1,0:T(8,128)S(1)}, f32[1,32,128]{2,1,0:T(8,128)S(1)}, u32[]{:S(2)}, u32[]{:S(2)}) collective-permute-start(f32[1,32,128]{2,1,0:T(8,128)S(1)} %copy.418), channel_id=1, source_target_pairs={{32,0},{64,32},{96,64},{128,96},{160,128},{192,160},{224,192},{256... | collective-permute-start | bytes 49160 | tf_op jit(solution)/shard_map/ppermute | solution.py:23
  13.8 15.1 %collective-permute-start = (f32[1,32,128]{2,1,0:T(8,128)S(1)}, f32[1,32,128]{2,1,0:T(8,128)S(1)}, u32[]{:S(2)}, u32[]{:S(2)}) collective-permute-start(f32[1,32,128]{2,1,0:T(8,128)S(1)} %copy.414), channel_id=1, source_target_pairs={{0,32},{32,64},{64,96},{96,128},{128,160},{160,192},{192,224},{224... | collective-permute-start | bytes 49160 | tf_op jit(solution)/shard_map/ppermute | solution.py:22
  16.5 18.4 %collective-permute-start.2 = (f32[1,32,128]{2,1,0:T(8,128)S(1)}, f32[1,32,128]{2,1,0:T(8,128)S(1)}, u32[]{:S(2)}, u32[]{:S(2)}) collective-permute-start(f32[1,32,128]{2,1,0:T(8,128)S(1)} %get-tuple-element.53), channel_id=1, source_target_pairs={{0,32},{32,64},{64,96},{96,128},{128,160},{160,192},{192,224},{224... | collective-permute-start | bytes 49160 | tf_op jit(solution)/shard_map/ppermute | solution.py:22
  18.7 16.2 %collective-permute-start.3 = (f32[1,32,128]{2,1,0:T(8,128)S(1)}, f32[1,32,128]{2,1,0:T(8,128)S(1)}, u32[]{:S(2)}, u32[]{:S(2)}) collective-permute-start(f32[1,32,128]{2,1,0:T(8,128)S(1)} %get-tuple-element.52), channel_id=1, source_target_pairs={{32,0},{64,32},{96,64},{128,96},{160,128},{192,160},{224,192},{256... | collective-permute-start | bytes 49160 | tf_op jit(solution)/shard_map/ppermute | solution.py:23
  27.0 30.7 %copy-start.6 = (f32[16,32,128]{2,1,0:T(8,128)S(1)}, f32[16,32,128]{2,1,0:T(8,128)}, u32[]{:S(2)}) copy-start(f32[16,32,128]{2,1,0:T(8,128)} %param.8) | copy-start | bytes 786436
  29.0 11.9 %collective-permute-start.5 = (f32[18,1,128]{2,1,0:T(1,128)S(1)}, f32[18,1,128]{2,1,0:T(1,128)S(1)}, u32[]{:S(2)}, u32[]{:S(2)}) collective-permute-start(f32[18,1,128]{2,1,0:T(1,128)S(1)} %get-tuple-element.43), channel_id=1, source_target_pairs={{1,0},{2,1},{3,2},{4,3},{5,4},{6,5},{7,6},{9,8},{10,9},{11,10},{12... | collective-permute-start | bytes 27656 | tf_op jit(solution)/shard_map/ppermute | solution.py:23
  31.3 9.6 %collective-permute-start.4 = (f32[18,1,128]{2,1,0:T(1,128)S(1)}, f32[18,1,128]{2,1,0:T(1,128)S(1)}, u32[]{:S(2)}, u32[]{:S(2)}) collective-permute-start(f32[18,1,128]{2,1,0:T(1,128)S(1)} %get-tuple-element.42), channel_id=1, source_target_pairs={{0,1},{1,2},{2,3},{3,4},{4,5},{5,6},{6,7},{8,9},{9,10},{10,11},{11... | collective-permute-start | bytes 27656 | tf_op jit(solution)/shard_map/ppermute | solution.py:22
  34.9 10.6 %collective-permute-start.7 = (f32[18,1,128]{2,1,0:T(1,128)S(1)}, f32[18,1,128]{2,1,0:T(1,128)S(1)}, u32[]{:S(2)}, u32[]{:S(2)}) collective-permute-start(f32[18,1,128]{2,1,0:T(1,128)S(1)} %get-tuple-element.41), channel_id=1, source_target_pairs={{1,0},{2,1},{3,2},{4,3},{5,4},{6,5},{7,6},{9,8},{10,9},{11,10},{12... | collective-permute-start | bytes 27656 | tf_op jit(solution)/shard_map/ppermute | solution.py:23
  37.3 8.2 %collective-permute-start.6 = (f32[18,1,128]{2,1,0:T(1,128)S(1)}, f32[18,1,128]{2,1,0:T(1,128)S(1)}, u32[]{:S(2)}, u32[]{:S(2)}) collective-permute-start(f32[18,1,128]{2,1,0:T(1,128)S(1)} %get-tuple-element.40), channel_id=1, source_target_pairs={{0,1},{1,2},{2,3},{3,4},{4,5},{5,6},{6,7},{8,9},{9,10},{10,11},{11... | collective-permute-start | bytes 27656 | tf_op jit(solution)/shard_map/ppermute | solution.py:22
  41.1 10.0 %collective-permute-start.9 = (f32[18,34,1]{2,1,0:T(8,128)S(1)}, f32[18,34,1]{2,1,0:T(8,128)S(1)}, u32[]{:S(2)}, u32[]{:S(2)}) collective-permute-start(f32[18,34,1]{2,1,0:T(8,128)S(1)} %get-tuple-element.31), channel_id=1, source_target_pairs={{8,0},{16,8},{24,16},{9,1},{17,9},{25,17},{10,2},{18,10},{26,18},{... | collective-permute-start | bytes 7352 | tf_op jit(solution)/shard_map/ppermute | solution.py:23
  43.1 8.8 %collective-permute-start.8 = (f32[18,34,1]{2,1,0:T(8,128)S(1)}, f32[18,34,1]{2,1,0:T(8,128)S(1)}, u32[]{:S(2)}, u32[]{:S(2)}) collective-permute-start(f32[18,34,1]{2,1,0:T(8,128)S(1)} %get-tuple-element.30), channel_id=1, source_target_pairs={{0,8},{8,16},{16,24},{1,9},{9,17},{17,25},{2,10},{10,18},{18,26},{... | collective-permute-start | bytes 7352 | tf_op jit(solution)/shard_map/ppermute | solution.py:22
  45.7 8.2 %collective-permute-start.11 = (f32[18,34,1]{2,1,0:T(8,128)S(1)}, f32[18,34,1]{2,1,0:T(8,128)S(1)}, u32[]{:S(2)}, u32[]{:S(2)}) collective-permute-start(f32[18,34,1]{2,1,0:T(8,128)S(1)} %get-tuple-element.29), channel_id=1, source_target_pairs={{8,0},{16,8},{24,16},{9,1},{17,9},{25,17},{10,2},{18,10},{26,18},{... | collective-permute-start | bytes 7352 | tf_op jit(solution)/shard_map/ppermute | solution.py:23
  48.9 8.8 %collective-permute-start.10 = (f32[18,34,1]{2,1,0:T(8,128)S(1)}, f32[18,34,1]{2,1,0:T(8,128)S(1)}, u32[]{:S(2)}, u32[]{:S(2)}) collective-permute-start(f32[18,34,1]{2,1,0:T(8,128)S(1)} %get-tuple-element.28), channel_id=1, source_target_pairs={{0,8},{8,16},{16,24},{1,9},{9,17},{17,25},{2,10},{10,18},{18,26},{... | collective-permute-start | bytes 7352 | tf_op jit(solution)/shard_map/ppermute | solution.py:22
  58.9 137.0 %copy-start.2 = (f32[16,32,128]{2,1,0:T(8,128)}, f32[16,32,128]{2,1,0:T(8,128)S(1)}, u32[]{:S(2)}) copy-start(f32[16,32,128]{2,1,0:T(8,128)S(1)} %get-tuple-element.19) | copy-start | bytes 786436
  58.9 16.0 %copy-start.16 = (f32[2,4,1,1,1,1]{1,0,5,4,3,2:T(2,128)S(1)}, f32[2,4,1,1,1,1]{1,0,5,4,3,2:T(2,128)}, u32[]{:S(2)}) copy-start(f32[2,4,1,1,1,1]{1,0,5,4,3,2:T(2,128)} %constant.102) | copy-start | bytes 100
  80.0 90.8 %copy-start.13 = (f32[4,2,1,1,1,1]{0,1,5,4,3,2:T(2,128)S(1)}, f32[4,2,1,1,1,1]{0,1,5,4,3,2:T(2,128)}, u32[]{:S(2)}) copy-start(f32[4,2,1,1,1,1]{0,1,5,4,3,2:T(2,128)} %constant.103) | copy-start | bytes 100
  82.6 5.1 %all-to-all-start = ((bf16[4,2,1024]{2,1,0:T(2,128)(2,1)}), bf16[4,2,1024]{2,1,0:T(2,128)(2,1)S(1)}, u32[]{:S(2)}, u32[]{:S(2)}) async-start(bf16[4,2,1024]{2,1,0:T(2,128)(2,1)} %reshape.214), calls=%async_computation | async-start | bytes 32768 | tf_op jit(solution)/shard_map/all_to_all | solution.py:142
  85.9 63.0 %copy-start.19 = (s32[128]{0:T(128)}, s32[128]{0:T(128)S(1)}, u32[]{:S(2)}) copy-start(s32[128]{0:T(128)S(1)} %iota_add_fusion.1) | copy-start | bytes 1540
  90.7 14.1 %all-to-all-start.1 = ((bf16[8,2,512]{2,1,0:T(2,128)(2,1)}), bf16[8,2,512]{2,1,0:T(2,128)(2,1)S(1)}, u32[]{:S(2)}, u32[]{:S(2)}) async-start(bf16[8,2,512]{2,1,0:T(2,128)(2,1)} %reshape.216), calls=%async_computation.1 | async-start | bytes 32768 | tf_op jit(solution)/shard_map/all_to_all | solution.py:146
  98.5 40.7 %copy-start.18 = (f32[32]{0:T(128)}, f32[32]{0:T(128)S(1)}, u32[]{:S(2)}) copy-start(f32[32]{0:T(128)S(1)} %multiply_subtract_fusion) | copy-start | bytes 388
  106.2 16.3 %all-to-all-start.2 = ((bf16[2,128,32]{2,0,1:T(2,128)(2,1)}), bf16[2,128,32]{2,0,1:T(2,128)(2,1)S(1)}, u32[]{:S(2)}, u32[]{:S(2)}) async-start(bf16[2,128,32]{2,0,1:T(2,128)(2,1)} %copy.434), calls=%async_computation.2 | async-start | bytes 131072 | tf_op jit(solution)/shard_map/all_to_all | solution.py:152
  115.4 20.4 %collective-permute-start.13 = (f32[1,32,128]{2,1,0:T(8,128)S(1)}, f32[1,32,128]{2,1,0:T(8,128)S(1)}, u32[]{:S(2)}, u32[]{:S(2)}) collective-permute-start(f32[1,32,128]{2,1,0:T(8,128)S(1)} %get-tuple-element.51), channel_id=1, source_target_pairs={{32,0},{64,32},{96,64},{128,96},{160,128},{192,160},{224,192},{256... | collective-permute-start | bytes 49160 | tf_op jit(solution)/shard_map/ppermute | solution.py:23
  120.2 15.6 %collective-permute-start.12 = (f32[1,32,128]{2,1,0:T(8,128)S(1)}, f32[1,32,128]{2,1,0:T(8,128)S(1)}, u32[]{:S(2)}, u32[]{:S(2)}) collective-permute-start(f32[1,32,128]{2,1,0:T(8,128)S(1)} %get-tuple-element.50), channel_id=1, source_target_pairs={{0,32},{32,64},{64,96},{96,128},{128,160},{160,192},{192,224},{224... | collective-permute-start | bytes 49160 | tf_op jit(solution)/shard_map/ppermute | solution.py:22
  125.1 17.7 %all-to-all-start.3 = ((bf16[128,2,32]{2,1,0:T(2,128)(2,1)}), bf16[128,2,32]{2,1,0:T(2,128)(2,1)S(1)}, u32[]{:S(2)}, u32[]{:S(2)}) async-start(bf16[128,2,32]{2,1,0:T(2,128)(2,1)} %copy.438), calls=%async_computation.3 | async-start | bytes 131072 | tf_op jit(solution)/shard_map/all_to_all | solution.py:175
  135.8 13.0 %collective-permute-start.15 = (f32[18,1,128]{2,1,0:T(1,128)S(1)}, f32[18,1,128]{2,1,0:T(1,128)S(1)}, u32[]{:S(2)}, u32[]{:S(2)}) collective-permute-start(f32[18,1,128]{2,1,0:T(1,128)S(1)} %get-tuple-element.39), channel_id=1, source_target_pairs={{1,0},{2,1},{3,2},{4,3},{5,4},{6,5},{7,6},{9,8},{10,9},{11,10},{12... | collective-permute-start | bytes 27656 | tf_op jit(solution)/shard_map/ppermute | solution.py:23
  139.1 9.7 %collective-permute-start.14 = (f32[18,1,128]{2,1,0:T(1,128)S(1)}, f32[18,1,128]{2,1,0:T(1,128)S(1)}, u32[]{:S(2)}, u32[]{:S(2)}) collective-permute-start(f32[18,1,128]{2,1,0:T(1,128)S(1)} %get-tuple-element.38), channel_id=1, source_target_pairs={{0,1},{1,2},{2,3},{3,4},{4,5},{5,6},{6,7},{8,9},{9,10},{10,11},{11... | collective-permute-start | bytes 27656 | tf_op jit(solution)/shard_map/ppermute | solution.py:22
  144.2 11.0 %all-to-all-start.4 = ((bf16[8,2,512]{2,1,0:T(2,128)(2,1)}), bf16[8,2,512]{2,1,0:T(2,128)(2,1)S(1)}, u32[]{:S(2)}, u32[]{:S(2)}) async-start(bf16[8,2,512]{2,1,0:T(2,128)(2,1)} %reshape.218), calls=%async_computation.4 | async-start | bytes 32768 | tf_op jit(solution)/shard_map/all_to_all | solution.py:179
  148.9 47.1 %copy-start.11 = (f32[18,1,128]{2,1,0:T(1,128)}, f32[18,1,128]{2,1,0:T(1,128)S(1)}, u32[]{:S(2)}) copy-start(f32[18,1,128]{2,1,0:T(1,128)S(1)} %collective-permute-done.15) | copy-start | bytes 27652
  148.9 47.1 %copy-start.12 = (f32[18,1,128]{2,1,0:T(1,128)}, f32[18,1,128]{2,1,0:T(1,128)S(1)}, u32[]{:S(2)}) copy-start(f32[18,1,128]{2,1,0:T(1,128)S(1)} %collective-permute-done.14) | copy-start | bytes 27652
  158.2 10.5 %all-to-all-start.5 = ((bf16[4,2,1024]{2,1,0:T(2,128)(2,1)}), bf16[4,2,1024]{2,1,0:T(2,128)(2,1)S(1)}, u32[]{:S(2)}, u32[]{:S(2)}) async-start(bf16[4,2,1024]{2,1,0:T(2,128)(2,1)} %reshape.220), calls=%async_computation.5 | async-start | bytes 32768 | tf_op jit(solution)/shard_map/all_to_all | solution.py:181
  163.7 32.2 %collective-permute-start.17 = (f32[18,34,1]{2,1,0:T(8,128)}, f32[18,34,1]{2,1,0:T(8,128)}, u32[]{:S(2)}, u32[]{:S(2)}) collective-permute-start(f32[18,34,1]{2,1,0:T(8,128)} %get-tuple-element.27), channel_id=1, source_target_pairs={{8,0},{16,8},{24,16},{9,1},{17,9},{25,17},{10,2},{18,10},{26,18},{... | collective-permute-start | bytes 7352 | tf_op jit(solution)/shard_map/ppermute | solution.py:23
  165.7 30.2 %collective-permute-start.16 = (f32[18,34,1]{2,1,0:T(8,128)}, f32[18,34,1]{2,1,0:T(8,128)}, u32[]{:S(2)}, u32[]{:S(2)}) collective-permute-start(f32[18,34,1]{2,1,0:T(8,128)} %get-tuple-element.26), channel_id=1, source_target_pairs={{0,8},{8,16},{16,24},{1,9},{9,17},{17,25},{2,10},{10,18},{18,26},{... | collective-permute-start | bytes 7352 | tf_op jit(solution)/shard_map/ppermute | solution.py:22
  172.2 23.7 %copy-start.4 = (f32[16,32,128]{2,1,0:T(8,128)S(1)}, f32[16,32,128]{2,1,0:T(8,128)}, u32[]{:S(2)}) copy-start(f32[16,32,128]{2,1,0:T(8,128)} %get-tuple-element.18) | copy-start | bytes 786436
  195.9 30.3 %copy-start.8 = (f32[16,32,128]{2,1,0:T(8,128)}, f32[16,32,128]{2,1,0:T(8,128)S(1)}, u32[]{:S(2)}) copy-start(f32[16,32,128]{2,1,0:T(8,128)S(1)} %reshape.198) | copy-start | bytes 786436
  197.6 6.8 %collective-permute-start.19 = (f32[1,32,128]{2,1,0:T(8,128)S(1)}, f32[1,32,128]{2,1,0:T(8,128)S(1)}, u32[]{:S(2)}, u32[]{:S(2)}) collective-permute-start(f32[1,32,128]{2,1,0:T(8,128)S(1)} %get-tuple-element.49), channel_id=1, source_target_pairs={{32,0},{64,32},{96,64},{128,96},{160,128},{192,160},{224,192},{256... | collective-permute-start | bytes 49160 | tf_op jit(solution)/shard_map/ppermute | solution.py:23
  201.5 8.6 %collective-permute-start.18 = (f32[1,32,128]{2,1,0:T(8,128)S(1)}, f32[1,32,128]{2,1,0:T(8,128)S(1)}, u32[]{:S(2)}, u32[]{:S(2)}) collective-permute-start(f32[1,32,128]{2,1,0:T(8,128)S(1)} %get-tuple-element.48), channel_id=1, source_target_pairs={{0,32},{32,64},{64,96},{96,128},{128,160},{160,192},{192,224},{224... | collective-permute-start | bytes 49160 | tf_op jit(solution)/shard_map/ppermute | solution.py:22
  210.1 6.0 %collective-permute-start.21 = (f32[18,1,128]{2,1,0:T(1,128)S(1)}, f32[18,1,128]{2,1,0:T(1,128)S(1)}, u32[]{:S(2)}, u32[]{:S(2)}) collective-permute-start(f32[18,1,128]{2,1,0:T(1,128)S(1)} %get-tuple-element.37), channel_id=1, source_target_pairs={{1,0},{2,1},{3,2},{4,3},{5,4},{6,5},{7,6},{9,8},{10,9},{11,10},{12... | collective-permute-start | bytes 27656 | tf_op jit(solution)/shard_map/ppermute | solution.py:23
  213.5 5.6 %collective-permute-start.20 = (f32[18,1,128]{2,1,0:T(1,128)S(1)}, f32[18,1,128]{2,1,0:T(1,128)S(1)}, u32[]{:S(2)}, u32[]{:S(2)}) collective-permute-start(f32[18,1,128]{2,1,0:T(1,128)S(1)} %get-tuple-element.36), channel_id=1, source_target_pairs={{0,1},{1,2},{2,3},{3,4},{4,5},{5,6},{6,7},{8,9},{9,10},{10,11},{11... | collective-permute-start | bytes 27656 | tf_op jit(solution)/shard_map/ppermute | solution.py:22
  219.2 6.9 %collective-permute-start.23 = (f32[18,34,1]{2,1,0:T(8,128)S(1)}, f32[18,34,1]{2,1,0:T(8,128)S(1)}, u32[]{:S(2)}, u32[]{:S(2)}) collective-permute-start(f32[18,34,1]{2,1,0:T(8,128)S(1)} %get-tuple-element.25), channel_id=1, source_target_pairs={{8,0},{16,8},{24,16},{9,1},{17,9},{25,17},{10,2},{18,10},{26,18},{... | collective-permute-start | bytes 7352 | tf_op jit(solution)/shard_map/ppermute | solution.py:23
  221.2 8.8 %collective-permute-start.22 = (f32[18,34,1]{2,1,0:T(8,128)S(1)}, f32[18,34,1]{2,1,0:T(8,128)S(1)}, u32[]{:S(2)}, u32[]{:S(2)}) collective-permute-start(f32[18,34,1]{2,1,0:T(8,128)S(1)} %get-tuple-element.24), channel_id=1, source_target_pairs={{0,8},{8,16},{16,24},{1,9},{9,17},{17,25},{2,10},{10,18},{18,26},{... | collective-permute-start | bytes 7352 | tf_op jit(solution)/shard_map/ppermute | solution.py:22
  231.4 0.7 copy-start.10
  232.1 16.0 %copy-start.17 = (f32[2,4,1,1,1,1]{1,0,5,4,3,2:T(2,128)S(1)}, f32[2,4,1,1,1,1]{1,0,5,4,3,2:T(2,128)}, u32[]{:S(2)}) copy-start(f32[2,4,1,1,1,1]{1,0,5,4,3,2:T(2,128)} %constant.102) | copy-start | bytes 100
  277.4 15.2 %all-to-all-start.8 = ((bf16[2,128,32]{2,0,1:T(2,128)(2,1)}), bf16[2,128,32]{2,0,1:T(2,128)(2,1)S(1)}, u32[]{:S(2)}, u32[]{:S(2)}) async-start(bf16[2,128,32]{2,0,1:T(2,128)(2,1)} %copy.462), calls=%async_computation.8 | async-start | bytes 131072 | tf_op jit(solution)/shard_map/all_to_all | solution.py:152
  285.5 21.4 %collective-permute-start.25 = (f32[1,32,128]{2,1,0:T(8,128)S(1)}, f32[1,32,128]{2,1,0:T(8,128)S(1)}, u32[]{:S(2)}, u32[]{:S(2)}) collective-permute-start(f32[1,32,128]{2,1,0:T(8,128)S(1)} %get-tuple-element.47), channel_id=1, source_target_pairs={{32,0},{64,32},{96,64},{128,96},{160,128},{192,160},{224,192},{256... | collective-permute-start | bytes 49160 | tf_op jit(solution)/shard_map/ppermute | solution.py:23
  290.4 16.5 %collective-permute-start.24 = (f32[1,32,128]{2,1,0:T(8,128)S(1)}, f32[1,32,128]{2,1,0:T(8,128)S(1)}, u32[]{:S(2)}, u32[]{:S(2)}) collective-permute-start(f32[1,32,128]{2,1,0:T(8,128)S(1)} %get-tuple-element.46), channel_id=1, source_target_pairs={{0,32},{32,64},{64,96},{96,128},{128,160},{160,192},{192,224},{224... | collective-permute-start | bytes 49160 | tf_op jit(solution)/shard_map/ppermute | solution.py:22
  296.5 17.5 %all-to-all-start.9 = ((bf16[128,2,32]{2,1,0:T(2,128)(2,1)}), bf16[128,2,32]{2,1,0:T(2,128)(2,1)S(1)}, u32[]{:S(2)}, u32[]{:S(2)}) async-start(bf16[128,2,32]{2,1,0:T(2,128)(2,1)} %copy.466), calls=%async_computation.9 | async-start | bytes 131072 | tf_op jit(solution)/shard_map/all_to_all | solution.py:175
  306.9 13.7 %collective-permute-start.27 = (f32[18,1,128]{2,1,0:T(1,128)S(1)}, f32[18,1,128]{2,1,0:T(1,128)S(1)}, u32[]{:S(2)}, u32[]{:S(2)}) collective-permute-start(f32[18,1,128]{2,1,0:T(1,128)S(1)} %get-tuple-element.35), channel_id=1, source_target_pairs={{1,0},{2,1},{3,2},{4,3},{5,4},{6,5},{7,6},{9,8},{10,9},{11,10},{12... | collective-permute-start | bytes 27656 | tf_op jit(solution)/shard_map/ppermute | solution.py:23
  310.3 10.4 %collective-permute-start.26 = (f32[18,1,128]{2,1,0:T(1,128)S(1)}, f32[18,1,128]{2,1,0:T(1,128)S(1)}, u32[]{:S(2)}, u32[]{:S(2)}) collective-permute-start(f32[18,1,128]{2,1,0:T(1,128)S(1)} %get-tuple-element.34), channel_id=1, source_target_pairs={{0,1},{1,2},{2,3},{3,4},{4,5},{5,6},{6,7},{8,9},{9,10},{10,11},{11... | collective-permute-start | bytes 27656 | tf_op jit(solution)/shard_map/ppermute | solution.py:22
  316.0 11.0 %all-to-all-start.10 = ((bf16[8,2,512]{2,1,0:T(2,128)(2,1)}), bf16[8,2,512]{2,1,0:T(2,128)(2,1)S(1)}, u32[]{:S(2)}, u32[]{:S(2)}) async-start(bf16[8,2,512]{2,1,0:T(2,128)(2,1)} %reshape.226), calls=%async_computation.10 | async-start | bytes 32768 | tf_op jit(solution)/shard_map/all_to_all | solution.py:179
  330.0 10.7 %all-to-all-start.11 = ((bf16[4,2,1024]{2,1,0:T(2,128)(2,1)}), bf16[4,2,1024]{2,1,0:T(2,128)(2,1)S(1)}, u32[]{:S(2)}, u32[]{:S(2)}) async-start(bf16[4,2,1024]{2,1,0:T(2,128)(2,1)} %reshape.228), calls=%async_computation.11 | async-start | bytes 32768 | tf_op jit(solution)/shard_map/all_to_all | solution.py:181
  335.5 35.2 %collective-permute-start.29 = (f32[18,34,1]{2,1,0:T(8,128)}, f32[18,34,1]{2,1,0:T(8,128)}, u32[]{:S(2)}, u32[]{:S(2)}) collective-permute-start(f32[18,34,1]{2,1,0:T(8,128)} %get-tuple-element.23), channel_id=1, source_target_pairs={{8,0},{16,8},{24,16},{9,1},{17,9},{25,17},{10,2},{18,10},{26,18},{... | collective-permute-start | bytes 7352 | tf_op jit(solution)/shard_map/ppermute | solution.py:23
  337.5 33.2 %collective-permute-start.28 = (f32[18,34,1]{2,1,0:T(8,128)}, f32[18,34,1]{2,1,0:T(8,128)}, u32[]{:S(2)}, u32[]{:S(2)}) collective-permute-start(f32[18,34,1]{2,1,0:T(8,128)} %get-tuple-element.22), channel_id=1, source_target_pairs={{0,8},{8,16},{16,24},{1,9},{9,17},{17,25},{2,10},{10,18},{18,26},{... | collective-permute-start | bytes 7352 | tf_op jit(solution)/shard_map/ppermute | solution.py:22
  345.6 25.1 %copy-start.3 = (f32[16,32,128]{2,1,0:T(8,128)S(1)}, f32[16,32,128]{2,1,0:T(8,128)}, u32[]{:S(2)}) copy-start(f32[16,32,128]{2,1,0:T(8,128)} %copy-done.2) | copy-start | bytes 786436
  345.6 25.1 %copy-start.5 = (f32[16,32,128]{2,1,0:T(8,128)S(1)}, f32[16,32,128]{2,1,0:T(8,128)}, u32[]{:S(2)}) copy-start(f32[16,32,128]{2,1,0:T(8,128)} %get-tuple-element.18) | copy-start | bytes 786436
  361.9 8.9 %copy-start.9 = (f32[16,32,128]{2,1,0:T(8,128)S(1)}, f32[16,32,128]{2,1,0:T(8,128)}, u32[]{:S(2)}) copy-start(f32[16,32,128]{2,1,0:T(8,128)} %copy-done.8) | copy-start | bytes 786436
  361.9 43.7 %copy-start.7 = (f32[16,32,128]{2,1,0:T(8,128)S(1)}, f32[16,32,128]{2,1,0:T(8,128)}, u32[]{:S(2)}) copy-start(f32[16,32,128]{2,1,0:T(8,128)} %param.8) | copy-start | bytes 786436
  373.1 33.6 %copy-start = (f32[16,32,128]{2,1,0:T(8,128)}, f32[16,32,128]{2,1,0:T(8,128)S(1)}, u32[]{:S(2)}) copy-start(f32[16,32,128]{2,1,0:T(8,128)S(1)} %fusion.45) | copy-start | bytes 786436
  373.1 6.8 %collective-permute-start.31 = (f32[1,32,128]{2,1,0:T(8,128)S(1)}, f32[1,32,128]{2,1,0:T(8,128)S(1)}, u32[]{:S(2)}, u32[]{:S(2)}) collective-permute-start(f32[1,32,128]{2,1,0:T(8,128)S(1)} %get-tuple-element.45), channel_id=1, source_target_pairs={{32,0},{64,32},{96,64},{128,96},{160,128},{192,160},{224,192},{256... | collective-permute-start | bytes 49160 | tf_op jit(solution)/shard_map/ppermute | solution.py:23
  377.0 8.6 %collective-permute-start.30 = (f32[1,32,128]{2,1,0:T(8,128)S(1)}, f32[1,32,128]{2,1,0:T(8,128)S(1)}, u32[]{:S(2)}, u32[]{:S(2)}) collective-permute-start(f32[1,32,128]{2,1,0:T(8,128)S(1)} %get-tuple-element.44), channel_id=1, source_target_pairs={{0,32},{32,64},{64,96},{96,128},{128,160},{160,192},{192,224},{224... | collective-permute-start | bytes 49160 | tf_op jit(solution)/shard_map/ppermute | solution.py:22
  385.7 5.9 %collective-permute-start.33 = (f32[18,1,128]{2,1,0:T(1,128)S(1)}, f32[18,1,128]{2,1,0:T(1,128)S(1)}, u32[]{:S(2)}, u32[]{:S(2)}) collective-permute-start(f32[18,1,128]{2,1,0:T(1,128)S(1)} %get-tuple-element.33), channel_id=1, source_target_pairs={{1,0},{2,1},{3,2},{4,3},{5,4},{6,5},{7,6},{9,8},{10,9},{11,10},{12... | collective-permute-start | bytes 27656 | tf_op jit(solution)/shard_map/ppermute | solution.py:23
  389.0 5.6 %collective-permute-start.32 = (f32[18,1,128]{2,1,0:T(1,128)S(1)}, f32[18,1,128]{2,1,0:T(1,128)S(1)}, u32[]{:S(2)}, u32[]{:S(2)}) collective-permute-start(f32[18,1,128]{2,1,0:T(1,128)S(1)} %get-tuple-element.32), channel_id=1, source_target_pairs={{0,1},{1,2},{2,3},{3,4},{4,5},{5,6},{6,7},{8,9},{9,10},{10,11},{11... | collective-permute-start | bytes 27656 | tf_op jit(solution)/shard_map/ppermute | solution.py:22
  394.8 6.9 %collective-permute-start.35 = (f32[18,34,1]{2,1,0:T(8,128)S(1)}, f32[18,34,1]{2,1,0:T(8,128)S(1)}, u32[]{:S(2)}, u32[]{:S(2)}) collective-permute-start(f32[18,34,1]{2,1,0:T(8,128)S(1)} %get-tuple-element.21), channel_id=1, source_target_pairs={{8,0},{16,8},{24,16},{9,1},{17,9},{25,17},{10,2},{18,10},{26,18},{... | collective-permute-start | bytes 7352 | tf_op jit(solution)/shard_map/ppermute | solution.py:23
  396.7 8.8 %collective-permute-start.34 = (f32[18,34,1]{2,1,0:T(8,128)S(1)}, f32[18,34,1]{2,1,0:T(8,128)S(1)}, u32[]{:S(2)}, u32[]{:S(2)}) collective-permute-start(f32[18,34,1]{2,1,0:T(8,128)S(1)} %get-tuple-element.20), channel_id=1, source_target_pairs={{0,8},{8,16},{16,24},{1,9},{9,17},{17,25},{2,10},{10,18},{18,26},{... | collective-permute-start | bytes 7352 | tf_op jit(solution)/shard_map/ppermute | solution.py:22
  (2 other events, 1.2 us)
where the time goes:
time: 413 us; the launch traced here: 407 us
  starting transfers between devices  180 us (44%)
  local copies, waits for them, and re-layouts  76.9 us (19%)
  waiting for transfers between devices  58.2 us (14%)
  matrix products  57.7 us (14%)
  blocking collectives  16.9 us (4%)
  other arithmetic  13.9 us (3%)
    ppermute x18, starting transfers between devices, extended(): after = lax.ppermute(first, axis, down)  65.4 us
    ppermute x18, starting transfers between devices, extended(): before = lax.ppermute(last, axis, up)  46.9 us
    reshape x4, local copies, waits for them, and re-layouts, restrict_field(): blocks = field.reshape(count_x, 4, count_z, 4, count_y, 4)  31.9 us
    dot_general x2, matrix products, prolong_field(): jnp.einsum('kc,pizjyc->pizjyk', matrix, blocks, precision=lax.Precision.H...  31.7 us
    ppermute x18, waiting for transfers between devices, extended(): before = lax.ppermute(last, axis, up)  29.7 us
    all_to_all x2, starting transfers between devices, coarse_correction(): lax.all_to_all(pencil, ('bx', 'by'), split_axis=0, concat_axis=1, tiled=T...  21 us
    all_to_all x2, starting transfers between devices, coarse_correction(): lax.all_to_all(pencil, ('bx', 'by'), split_axis=1, concat_axis=0, tiled=T...  17.3 us
    reshape x2, local copies, waits for them, and re-layouts, prolong_field(): return blocks.reshape(4 * count_x, 4 * count_z, 4 * count_y)  17 us
  transfers between devices with their start and end apart: 46, of which 18 were waited for; matrix products, arithmetic and copies ran while one was open for 18% of the time, Pallas kernels for 0%

commit v1 on v0

v1 whole, which is shorter than its diff:
```python
import math

import jax
import jax.numpy as jnp
import numpy as np
from jax import lax
from jax.experimental import pallas as pl
from jax.experimental.pallas import tpu as pltpu
from jax.sharding import PartitionSpec as P

CYCLES = 2
DAMPING = 0.6666666666666666
NBX, NBY, NBZ = 16, 4, 8
CX, CZ, CY = 128, 128, 256
F32, BF16 = jnp.float32, jnp.bfloat16
MESH = pl.DeviceIdType.MESH
OFFSETS = sorted(
    ((a, b) for a in range(4) for b in range(4) if (a, b) != (0, 0)),
    key=lambda o: -(min(o[0], 4 - o[0]) + 2 * min(o[1], 4 - o[1])),
)


def rounded(value):
    return np.asarray(value, dtype=np.float64).astype(np.float32).astype(jnp.bfloat16)


def sine(count):
    index = np.arange(1, count + 1, dtype=np.float64)
    table = np.sin(np.outer(index, index) * (math.pi / (count + 1))) * math.sqrt(2.0 / (count + 1))
    return rounded(table).astype(np.float64)


def spectrum(count):
    return 2.0 - 2.0 * np.cos(np.arange(1, count + 1) * (math.pi / (count + 1)))


def tables():
    sine_x, sine_z, sine_y = sine(CX), sine(CZ), sine(CY)
    steps = np.array([[3.0, 2.0, 1.0, 0.0], [0.0, 1.0, 2.0, 3.0]])
    restrict_y = np.kron(np.eye(32), steps)
    restrict_y = np.concatenate([restrict_y, restrict_y], axis=1)
    restrict_z = np.kron(np.eye(64), steps).T
    prolong_z = np.concatenate([restrict_z, restrict_z], axis=1)
    blocks = sine_x.reshape(CX, NBX, 8)
    forward_x = np.zeros((2, CX, NBX, 2, 8))
    inverse_x = np.zeros((NBX, 2, 8, 2, CX))
    for member in range(2):
        forward_x[member, :, :, member, :] = blocks
        inverse_x[:, member, :, member, :] = sine_x.reshape(NBX, 8, CX)
    prolong_y = np.kron(np.eye(CY // 2), steps / 3.0)
    spread = (sine_y @ prolong_y).reshape(CY, NBY, 128).transpose(1, 0, 2)
    high = rounded(spread)
    low = rounded(spread - high.astype(np.float64))
    spread = np.stack([high, low], axis=1)
    plane = (spectrum(CX)[:, None] + spectrum(CZ)[None, :]).astype(np.float32)
    return (
        rounded(restrict_y),
        rounded(restrict_z),
        rounded(prolong_z),
        rounded(sine_y).reshape(NBY, 64, CY),
        rounded(sine_z),
        rounded(forward_x.reshape(256, 256)),
        rounded(inverse_x.reshape(NBX, 16, 256)),
        spread,
        plane,
        spectrum(CY).astype(np.float32),
    )


def turn(values, block):
    values = list(values)
    for bit in (4, 2, 1):
        low = (block & bit) == 0
        for first in range(8):
            if first & bit:
                continue
            second = first | bit
            one, two = values[first], values[second]
            values[first] = jnp.where(low, one, pltpu.roll(two, 16 * bit, 1))
            values[second] = jnp.where(low, pltpu.roll(one, 128 - 16 * bit, 1), two)
    return values


def kernel(
    forcing_hbm, start_hbm, class_ref, coef, eigen_y, ry_hbm, rz_hbm, pz_hbm, sy_hbm, sz_hbm,
    fx_hbm, ix_hbm, sp_hbm, plane_hbm,
    out_hbm, resid_hbm,
    f, s, z, r, inner, kap, beta, base, diag, dinv, wx, wxb, wzl, wzh, wzb, wyl, wyh, wyb,
    xh, zh, yh, zsend, ysend, kx, kz, ky, kzsend, kysend,
    ry, rz, pz, sy, sz, fx, ix, sp, plane, invlam, fine, swap,
    c0, va, vsend, xg, vb, vbsend, c5, last,
    load_sem, halo_s, halo_r, kap_s, kap_r, y1_s, y1_r, z1_s, z1_r, x_s, x_r, z2_s, z2_r, y2_s, y2_r,
):
    ib, iy, iz = lax.axis_index("bx"), lax.axis_index("by"), lax.axis_index("bz")
    loads = [
        pltpu.make_async_copy(src, dst, load_sem.at[i])
        for i, (src, dst) in enumerate(
            [
                (start_hbm, s.at[0]), (forcing_hbm, f), (ry_hbm, ry), (rz_hbm, rz), (pz_hbm, pz),
                (sy_hbm.at[iy], sy), (sz_hbm, sz), (fx_hbm, fx), (ix_hbm.at[ib], ix),
                (sp_hbm.at[iy], sp), (plane_hbm, plane),
            ]
        )
    ]
    for load in loads:
        load.start()

    def x_peer(offset):
        return lax.rem(ib // 4 + offset[0], 4) * 4 + lax.rem(lax.rem(ib, 4) + offset[1], 4)

    def z_peer(offset):
        return lax.rem(iz + offset, NBZ)

    def y_peer(offset):
        return lax.rem(iy + offset, NBY)

    z_order = (4, 3, 5, 2, 6, 1, 7)
    y_order = (2, 3, 1)
    barrier = pltpu.get_barrier_semaphore()
    for offset in OFFSETS:
        pl.semaphore_signal(barrier, inc=1, device_id={"bx": x_peer(offset)}, device_id_type=MESH)
    for offset in z_order:
        pl.semaphore_signal(barrier, inc=1, device_id={"bz": z_peer(offset)}, device_id_type=MESH)
    for offset in y_order:
        pl.semaphore_signal(barrier, inc=1, device_id={"by": y_peer(offset)}, device_id_type=MESH)

    row = lax.broadcasted_iota(jnp.int32, (32, 128), 0)
    lane = lax.broadcasted_iota(jnp.int32, (32, 128), 1)
    spread_y = (lax.broadcasted_iota(jnp.int32, (32, 128), 1) // 4 == row).astype(F32).astype(BF16)
    tall = lax.broadcasted_iota(jnp.int32, (128, 32), 0) // 4
    spread_z = (tall == lax.broadcasted_iota(jnp.int32, (128, 32), 1)).astype(F32).astype(BF16)
    labels = class_ref[...].astype(F32).astype(BF16)
    labels = jnp.dot(labels, spread_y, preferred_element_type=F32).astype(BF16)
    labels = jnp.dot(spread_z, labels, preferred_element_type=F32)
    kappa = jnp.zeros((128, 128), F32)
    sigma = jnp.zeros((128, 128), F32)
    cubic = jnp.zeros((128, 128), F32)
    for index in range(16):
        hit = labels == float(index)
        kappa = jnp.where(hit, coef[0, index], kappa)
        sigma = jnp.where(hit, coef[1, index], sigma)
        cubic = jnp.where(hit, coef[2, index], cubic)
    kap[...] = kappa.reshape(4, 32, 128)
    base[...] = sigma.reshape(4, 32, 128)
    beta[...] = cubic.reshape(4, 32, 128)
    kysend[...] = jnp.transpose(pltpu.roll(kappa, 1, 1))[0:8]
    kzsend[0:4] = kap[:, 0, :]
    kzsend[4:8] = kap[:, 31, :]

    def pack(field, slot):
        wide = lax.broadcasted_iota(jnp.int32, (128, 128), 1)
        edge = jnp.zeros((128, 128), F32)
        for e in range(4):
            part = field[4 * e : 4 * e + 4].reshape(128, 128)
            edge = jnp.where(wide // 2 == e, pltpu.roll(part, 1 + 2 * e, 1), edge)
        ysend[slot] = jnp.transpose(edge)[0:8]
        zsend[slot, 0] = field[:, 0, :]
        zsend[slot, 1] = field[:, 31, :]

    xa, xb = lax.rem(ib + 15, NBX), lax.rem(ib + 1, NBX)
    ya, yb = lax.rem(iy + 3, NBY), lax.rem(iy + 1, NBY)
    za, zb = lax.rem(iz + 7, NBZ), lax.rem(iz + 1, NBZ)

    def remote(src, dst, send, recv, device):
        return pltpu.make_async_remote_copy(
            src_ref=src, dst_ref=dst, send_sem=send, recv_sem=recv, device_id=device, device_id_type=MESH
        )

    def halo(field, slot, kind):
        ss, rs = halo_s.at[kind], halo_r.at[kind]
        return [
            remote(field.at[0], xh.at[slot, 1], ss.at[0], rs.at[0], {"bx": xa}),
            remote(field.at[15], xh.at[slot, 0], ss.at[1], rs.at[1], {"bx": xb}),
            remote(zsend.at[slot, 0], zh.at[slot, 1], ss.at[2], rs.at[2], {"bz": za}),
            remote(zsend.at[slot, 1], zh.at[slot, 0], ss.at[3], rs.at[3], {"bz": zb}),
            remote(ysend.at[slot], yh.at[slot, 1], ss.at[4], rs.at[4], {"by": ya}),
            remote(ysend.at[slot], yh.at[slot, 0], ss.at[5], rs.at[5], {"by": yb}),
        ]

    loads[0].wait()
    pack(s.at[0], 0)
    kappa_copies = [
        remote(kap.at[0], kx.at[1], kap_s.at[0], kap_r.at[0], {"bx": xa}),
        remote(kap.at[3], kx.at[0], kap_s.at[1], kap_r.at[1], {"bx": xb}),
        remote(kzsend, kz.at[1], kap_s.at[2], kap_r.at[2], {"bz": za}),
        remote(kzsend, kz.at[0], kap_s.at[3], kap_r.at[3], {"bz": zb}),
        remote(kysend, ky.at[1], kap_s.at[4], kap_r.at[4], {"by": ya}),
        remote(kysend, ky.at[0], kap_s.at[5], kap_r.at[5], {"by": yb}),
    ]
    pl.semaphore_wait(barrier, len(OFFSETS) + len(z_order) + len(y_order))
    for copy in kappa_copies:
        copy.start()
    copies = halo(s.at[0], 0, 0)
    for copy in copies:
        copy.start()

    zero = jnp.zeros((32, 128), F32)
    for e in range(4):
        k = kap[e]
        first, second, third = (row % 4 == 0), (row % 4 == 3), (lane % 4 == 0)
        zl = jnp.where(row == 0, zero, jnp.where(first, pltpu.roll(k, 1, 0) + k, k))
        zu = jnp.where(row == 31, zero, jnp.where(second, pltpu.roll(k, 31, 0) + k, k))
        yl = jnp.where(lane == 0, zero, jnp.where(third, pltpu.roll(k, 1, 1) + k, k))
        yu = jnp.where(lane == 127, zero, jnp.where(lane % 4 == 3, pltpu.roll(k, 127, 1) + k, k))
        wzl[e], wzh[e], wyl[e], wyh[e] = zl, zu, yl, yu
        base[e] = base[e] + ((zl + zu) + (yl + yu))
        for j in range(4):
            if j > 0:
                wx[4 * e + j] = k
            elif e > 0:
                wx[4 * e] = kap[e - 1] + k
    wx[0] = zero
    wx[16] = zero

    def inner_sum(field):
        def step(e, carry):
            zl, zu, yl, yu = wzl[e], wzh[e], wyl[e], wyh[e]
            for j in range(4):
                x = 4 * e + j
                v = field[x]
                total = zl * pltpu.roll(v, 1, 0) + zu * pltpu.roll(v, 31, 0)
                total = total + yl * pltpu.roll(v, 1, 1) + yu * pltpu.roll(v, 127, 1)
                total = total + wx[x] * field[lax.rem(x + 15, 16)]
                total = total + wx[x + 1] * field[lax.rem(x + 1, 16)]
                inner[x] = total
            return carry

        lax.fori_loop(0, 4, step, 0)

    inner_sum(s.at[0])

    kbar, sbar = coef[0, 0], coef[1, 0]
    for index in range(1, 16):
        kbar, sbar = kbar + coef[0, index], sbar + coef[1, index]
    kbar, sbar = kbar * 0.0625, sbar * 0.0625
    loads[10].wait()
    mode = iy * 64 + iz * 8
    for member in range(2):
        for pair in range(4):
            value = kbar * (plane[...] + eigen_y[mode + 2 * pair + member]) + sbar
            invlam[pl.ds(member * 128, 128), pl.ds(pair * 128, 128)] = 1.0 / value

    def inside(flag):
        return jnp.where(flag, 1.0, 0.0).astype(F32)

    x_in = (inside(ib > 0), inside(ib < NBX - 1))
    z_in = (inside(iz > 0), inside(iz < NBZ - 1))
    y_in = (inside(iy > 0), inside(iy < NBY - 1))
    for copy in kappa_copies:
        copy.wait()
    row8 = lax.broadcasted_iota(jnp.int32, (8, 128), 0)
    ends = []
    for side, e in ((0, 0), (1, 3)):
        weight = kap[e] + kx[side] * x_in[side]
        wxb[side] = weight * x_in[side]
        ends.append(weight)
    low_y = jnp.transpose(ky[0])[:, 0:1]
    high_y = jnp.transpose(ky[1])[:, 1:2]
    wide = lax.broadcasted_iota(jnp.int32, (128, 128), 1)
    outer = jnp.where(wide == 0, y_in[0], jnp.where(wide == 127, y_in[1], 0.0))
    other = jnp.where(wide == 0, jnp.broadcast_to(low_y, (128, 128)), jnp.broadcast_to(high_y, (128, 128)))
    edge_y = (wide == 0) | (wide == 127)
    edge_y = jnp.where(edge_y, kap[...].reshape(128, 128) + other * outer, 0.0)
    wyb[...] = (edge_y * outer).reshape(4, 32, 128)
    base[...] = base[...] + edge_y.reshape(4, 32, 128)
    for e in range(4):
        low = jnp.where(row8 == 0, kap[e, 0:8, :] + kz[0, 4 + e : 5 + e, :] * z_in[0], 0.0)
        high = jnp.where(row8 == 7, kap[e, 24:32, :] + kz[1, e : e + 1, :] * z_in[1], 0.0)
        wzb[0, e] = low * z_in[0]
        wzb[1, e] = high * z_in[1]
        base[e, 0:8, :] = base[e, 0:8, :] + low
        base[e, 24:32, :] = base[e, 24:32, :] + high
    for x in range(16):
        below = ends[0] if x == 0 else wx[x]
        above = ends[1] if x == 15 else wx[x + 1]
        total = base[x // 4] + (below + above)
        diag[x] = total
        dinv[x] = DAMPING / total

    def outer_sum(slot):
        inner[0] = inner[0] + wxb[0] * xh[slot, 0]
        inner[15] = inner[15] + wxb[1] * xh[slot, 1]
        low_y, high_y = jnp.transpose(yh[slot, 0]), jnp.transpose(yh[slot, 1])
        wide = lax.broadcasted_iota(jnp.int32, (128, 128), 1)
        for e in range(4):
            low = jnp.broadcast_to(low_y[:, 2 * e : 2 * e + 1], (128, 128))
            high = jnp.broadcast_to(high_y[:, 2 * e + 1 : 2 * e + 2], (128, 128))
            other = jnp.where(wide == 0, low, high).reshape(4, 32, 128)
            weight = wyb[e]
            for j in range(4):
                x = 4 * e + j
                inner[x] = inner[x] + weight * other[j]
                inner[x, 0:8, :] = inner[x, 0:8, :] + wzb[0, e] * zh[slot, 0, x : x + 1, :]
                inner[x, 24:32, :] = inner[x, 24:32, :] + wzb[1, e] * zh[slot, 1, x : x + 1, :]

    def residual(field, store):
        def step(e, carry):
            cube = beta[e]
            planes = []
            for j in range(4):
                x = 4 * e + j
                v = field[x]
                value = (f[x] - (diag[x] * v - inner[x])) - cube * v * v * v
                store[x] = value
                planes.append(value)
            return carry

        lax.fori_loop(0, 4, step, 0)

    block = lax.broadcasted_iota(jnp.int32, (8, 128), 1) // 16
    loads[1].wait()
    for load in loads[2:10]:
        load.wait()

    for cycle in range(CYCLES):
        for copy in copies:
            copy.wait()
        field = s.at[cycle]
        outer_sum(2 * cycle)
        residual(field, r)

        for e in range(4):
            one, two, three, four = (r[4 * e + j] for j in range(4))
            for half, value in ((0, 3.0 * one + 2.0 * two + three), (1, two + 2.0 * three + 3.0 * four)):
                high = value.astype(BF16)
                at = pl.ds((2 * e + half) * 32, 32)
                fine[at, 0:128] = high
                fine[at, 128:256] = (value - high.astype(F32)).astype(BF16)
        value = lax.dot_general(ry[...], fine[...], (((1,), (1,)), ((), ())), preferred_element_type=F32)
        high = value.astype(BF16)
        low = (value - high.astype(F32)).astype(BF16)
        value = jnp.dot(high, rz[...], preferred_element_type=F32) + jnp.dot(
            low, rz[...], preferred_element_type=F32
        )
        c0[cycle, iy] = (value * (1.0 / 216.0)).astype(BF16)
        sends = [
            remote(c0.at[cycle, iy], c0.at[cycle, iy], y1_s.at[cycle, y_peer(o)], y1_r.at[cycle, iy], {"by": y_peer(o)})
            for o in y_order
        ]
        for copy in sends:
            copy.start()

        smooth = z.at[cycle]
        smooth[...] = r[...] * dinv[...]
        pack(smooth, 2 * cycle + 1)
        smooth_copies = halo(smooth, 2 * cycle + 1, 1)

        for o in y_order:
            p = y_peer(o)
            remote(c0.at[cycle, p], c0.at[cycle, p], y1_s.at[cycle, p], y1_r.at[cycle, p], {"by": p}).wait_recv()
        value = jnp.dot(sy[...], c0[cycle].reshape(CY, 128), preferred_element_type=F32)
        vsend[cycle] = value.reshape(8, 8, 128).astype(BF16)
        z_sends = [
            remote(vsend.at[cycle, z_peer(o)], va.at[cycle, iz], z1_s.at[cycle, z_peer(o)], z1_r.at[cycle, iz], {"bz": z_peer(o)})
            for o in z_order
        ]
        for copy in z_sends:
            copy.start()
        va[cycle, iz] = vsend[cycle, iz]
        for copy in smooth_copies:
            copy.start()
        inner_sum(smooth)
        for copy in sends:
            copy.wait_send()
        for o in z_order:
            p = z_peer(o)
            remote(vsend.at[cycle, p], va.at[cycle, p], z1_s.at[cycle, p], z1_r.at[cycle, p], {"bz": p}).wait_recv()
        parts = turn([va[cycle, i].astype(F32) for i in range(8)], block)
        value = jnp.concatenate(parts, axis=0).astype(BF16)
        swap[...] = jnp.dot(value, sz[...], preferred_element_type=F32)
        value = jnp.concatenate([swap[pl.ds(m, 8, stride=8), :] for m in range(8)], axis=0)
        xg[cycle, ib] = value.reshape(4, 16, 128).astype(BF16)
        x_sends = [
            remote(xg.at[cycle, ib], xg.at[cycle, ib], x_s.at[cycle, x_peer(o)], x_r.at[cycle, ib], {"bx": x_peer(o)})
            for o in OFFSETS
        ]
        for copy in x_sends:
            copy.start()
        for copy in z_sends:
            copy.wait_send()

        for copy in smooth_copies:
            copy.wait()
        outer_sum(2 * cycle + 1)
        s[cycle + 1] = s[cycle] + ((2.0 - DAMPING) * smooth[...] + dinv[...] * inner[...])

        for o in OFFSETS:
            p = x_peer(o)
            remote(xg.at[cycle, p], xg.at[cycle, p], x_s.at[cycle, p], x_r.at[cycle, p], {"bx": p}).wait_recv()
        parts = []
        for half in range(2):
            value = jnp.concatenate(
                [xg[cycle, :, 2 * half + i, :, :].reshape(256, 128) for i in range(2)], axis=1
            )
            value = jnp.dot(fx[...], value, preferred_element_type=F32)
            value = (value * invlam[:, 256 * half : 256 * half + 256]).astype(BF16)
            value = jnp.dot(ix[...], value, preferred_element_type=F32)
            parts += [value[:, 0:128], value[:, 128:256]]
        value = jnp.concatenate(parts, axis=0).astype(BF16)
        swap[...] = jnp.dot(value, sz[...], preferred_element_type=F32)
        parts = turn([swap[pl.ds(i, 8, stride=8), :] for i in range(8)], block)
        for i in range(8):
            vbsend[cycle, i] = parts[i].astype(BF16)
        z_sends = [
            remote(vbsend.at[cycle, z_peer(o)], vb.at[cycle, iz], z2_s.at[cycle, z_peer(o)], z2_r.at[cycle, iz], {"bz": z_peer(o)})
            for o in z_order
        ]
        for copy in z_sends:
            copy.start()
        vb[cycle, iz] = vbsend[cycle, iz]
        for copy in x_sends:
            copy.wait_send()
        for o in z_order:
            p = z_peer(o)
            remote(vbsend.at[cycle, p], vb.at[cycle, p], z2_s.at[cycle, p], z2_r.at[cycle, p], {"bz": p}).wait_recv()
        c5[cycle, iy] = vb[cycle].astype(F32).reshape(64, 128).astype(BF16)
        sends = [
            remote(c5.at[cycle, iy], c5.at[cycle, iy], y2_s.at[cycle, y_peer(o)], y2_r.at[cycle, iy], {"by": y_peer(o)})
            for o in y_order
        ]
        for copy in sends:
            copy.start()
        for copy in z_sends:
            copy.wait_send()
        for o in y_order:
            p = y_peer(o)
            remote(c5.at[cycle, p], c5.at[cycle, p], y2_s.at[cycle, p], y2_r.at[cycle, p], {"by": p}).wait_recv()

        modes = c5[cycle].reshape(CY, 128)
        over = (((0,), (0,)), ((), ()))
        value = lax.dot_general(modes, sp[0], over, preferred_element_type=F32) + lax.dot_general(
            modes, sp[1], over, preferred_element_type=F32
        )
        high = value.astype(BF16)
        low = (value - high.astype(F32)).astype(BF16)
        value = jnp.dot(pz[...], jnp.concatenate([high, low], axis=0), preferred_element_type=F32)
        value = (value * (1.0 / 3.0)).reshape(8, 32, 128)
        after = s.at[cycle + 1]
        for e in range(4):
            one, two = value[2 * e], value[2 * e + 1]
            mixed = (one, one * (2.0 / 3.0) + two * (1.0 / 3.0), one * (1.0 / 3.0) + two * (2.0 / 3.0), two)
            for j in range(4):
                after[4 * e + j] = after[4 * e + j] + mixed[j]
        pack(after, 2 * cycle + 2)
        copies = halo(after, 2 * cycle + 2, 0)
        for copy in copies:
            copy.start()
        for copy in sends:
            copy.wait_send()
        inner_sum(after)

    store = pltpu.make_async_copy(s.at[CYCLES], out_hbm, load_sem.at[0])
    store.start()
    for copy in copies:
        copy.wait()
    outer_sum(2 * CYCLES)
    residual(s.at[CYCLES], last)
    final = pltpu.make_async_copy(last, resid_hbm, load_sem.at[1])
    final.start()
    store.wait()
    final.wait()


def body(forcing, start, element_class_index, class_coef):
    consts = [jnp.asarray(t) for t in tables()]
    eigen_y = consts.pop()
    full, brick = (16, 32, 128), (4, 32, 128)
    vmem = pltpu.VMEM
    dma = pltpu.SemaphoreType.DMA
    scratch = (
        [vmem(full, F32), vmem((3,) + full, F32), vmem((2,) + full, F32), vmem(full, F32), vmem(full, F32)]
        + [vmem(brick, F32)] * 3
        + [vmem(full, F32)] * 2
        + [vmem((17, 32, 128), F32), vmem((2, 32, 128), F32)]
        + [vmem(brick, F32)] * 2
        + [vmem((2, 4, 8, 128), F32)]
        + [vmem(brick, F32)] * 3
        + [vmem((5, 2, 32, 128), F32), vmem((5, 2, 16, 128), F32), vmem((5, 2, 8, 128), F32)]
        + [vmem((5, 2, 16, 128), F32), vmem((5, 8, 128), F32)]
        + [vmem((2, 32, 128), F32), vmem((2, 8, 128), F32), vmem((2, 8, 128), F32)]
        + [vmem((8, 128), F32), vmem((8, 128), F32)]
        + [vmem((64, 256), BF16), vmem((256, 128), BF16), vmem((256, 256), BF16), vmem((64, 256), BF16)]
        + [vmem((128, 128), BF16), vmem((256, 256), BF16), vmem((16, 256), BF16), vmem((2, 256, 128), BF16)]
        + [vmem((128, 128), F32), vmem((256, 512), F32), vmem((256, 256), BF16), vmem((64, 128), F32)]
        + [vmem((2, 4, 64, 128), BF16), vmem((2, 8, 8, 128), BF16), vmem((2, 8, 8, 128), BF16)]
        + [vmem((2, 16, 4, 16, 128), BF16), vmem((2, 8, 8, 128), BF16), vmem((2, 8, 8, 128), BF16)]
        + [vmem((2, 4, 64, 128), BF16), vmem(full, F32)]
        + [dma((11,)), dma((2, 6)), dma((2, 6)), dma((6,)), dma((6,))]
        + [dma((2, 4))] * 2
        + [dma((2, 8))] * 2
        + [dma((2, 16))] * 2
        + [dma((2, 8))] * 2
        + [dma((2, 4))] * 2
    )
    anywhere = pl.BlockSpec(memory_space=pl.ANY)
    scalar = pl.BlockSpec(memory_space=pltpu.SMEM)
    shape = jax.ShapeDtypeStruct(full, F32)
    return pl.pallas_call(
        kernel,
        out_shape=(shape, shape),
        in_specs=[anywhere, anywhere, pl.BlockSpec(memory_space=pltpu.VMEM), scalar, scalar] + [anywhere] * 9,
        out_specs=(anywhere, anywhere),
        scratch_shapes=scratch,
        compiler_params=pltpu.CompilerParams(collective_id=0, has_side_effects=True),
        name="cycles",
    )(forcing, start, element_class_index.reshape(32, 32), class_coef, eigen_y, *consts)


def solution(mesh):
    spec = P("bx", "bz", "by")
    return jax.shard_map(
        body, mesh=mesh, in_specs=(spec, spec, spec, P()), out_specs=(spec, spec), check_vma=False
    )
```

time: 413 us -> 86.8 us (0.21)
  the two profiles are of different devices: /device:TPU:78 before, /device:TPU:1 now
where the time goes in v1:
time: 86.8 us; the launch traced here: 86.6 us
  Pallas kernels  83.6 us (96%)
  local copies, waits for them, and re-layouts  2.42 us (3%)
    pallas_call x1, Pallas kernels, body(): pl.pallas_call(kernel, out_shape=(shape, shape), in_specs=[anywhere, anyw...  83.6 us
    unnamed x4, local copies, waits for them, and re-layouts  2.42 us

profile of v1, /device:TPU:1, one launch (start us, length us, event | category | flops | bytes accessed | tf_op | source)
XLA Modules:
  0.0 86.6 jit_solution(3348129662821720724)
XLA Ops:
  0.6 83.6 %cycles.1 = (f32[16,32,128]{2,1,0:T(8,128)}, f32[16,32,128]{2,1,0:T(8,128)}) custom-call(f32[16,32,128]{2,1,0:T(8,128)} %forcing_hbm.1, f32[16,32,128]{2,1,0:T(8,128)} %start_hbm.1, s32[32,32]{1,0:T(8,128)} %bitcast.1, f32[3,16]{1,0:T(4,128)} %coef.1, f32[256]{0:T(256)} %constant.29.clone.eigen_y, bf16[64,256]{1,0:T(8,128)(2,1)} %constant.20.clone.ry_hbm, ...), custom_call_target="tpu_custom_call" | custom-call | tf_op jit(solution)/shard_map/cycles/pallas_call | solution.py:498
  84.2 0.0 copy-start
  84.2 1.7 %copy.18 = f32[16,32,128]{2,1,0:T(8,128)} copy(f32[16,32,128]{2,1,0:T(8,128)} %get-tuple-element.4) | data formatting | bytes 524288
  85.9 0.0 copy-done
  85.9 0.7 copy.19
Async XLA Ops:
  84.2 1.7 %copy-start = (f32[16,32,128]{2,1,0:T(8,128)S(1)}, f32[16,32,128]{2,1,0:T(8,128)}, u32[]{:S(2)}) copy-start(f32[16,32,128]{2,1,0:T(8,128)} %get-tuple-element.5) | copy-start | bytes 786436

commit v2 on v1

--- a/solution.py
+++ b/solution.py
@@ -20,6 +20,9 @@
 )
 
 
+PLANE = [(a, b) for b in (4, 3, 5, 2, 6, 1, 7, 0) for a in (2, 3, 1, 0) if (a, b) != (0, 0)]
+
+
 def rounded(value):
     return np.asarray(value, dtype=np.float64).astype(np.float32).astype(jnp.bfloat16)
 
@@ -34,34 +37,50 @@
     return 2.0 - 2.0 * np.cos(np.arange(1, count + 1) * (math.pi / (count + 1)))
 
 
+def split(value):
+    high = rounded(value)
+    return high, rounded(value - high.astype(np.float64))
+
+
 def tables():
     sine_x, sine_z, sine_y = sine(CX), sine(CZ), sine(CY)
     steps = np.array([[3.0, 2.0, 1.0, 0.0], [0.0, 1.0, 2.0, 3.0]])
-    restrict_y = np.kron(np.eye(32), steps)
-    restrict_y = np.concatenate([restrict_y, restrict_y], axis=1)
-    restrict_z = np.kron(np.eye(64), steps).T
-    prolong_z = np.concatenate([restrict_z, restrict_z], axis=1)
+    restrict_z = np.kron(np.eye(64), steps)
+    prolong_z = np.concatenate([restrict_z.T, restrict_z.T], axis=1)
     blocks = sine_x.reshape(CX, NBX, 8)
     forward_x = np.zeros((2, CX, NBX, 2, 8))
-    inverse_x = np.zeros((NBX, 2, 8, 2, CX))
+    inverse_x = np.zeros((NBX, 2, 16, 2, CX))
     for member in range(2):
         forward_x[member, :, :, member, :] = blocks
-        inverse_x[:, member, :, member, :] = sine_x.reshape(NBX, 8, CX)
-    prolong_y = np.kron(np.eye(CY // 2), steps / 3.0)
-    spread = (sine_y @ prolong_y).reshape(CY, NBY, 128).transpose(1, 0, 2)
-    high = rounded(spread)
-    low = rounded(spread - high.astype(np.float64))
-    spread = np.stack([high, low], axis=1)
+        inverse_x[:, member, :8, member, :] = sine_x.reshape(NBX, 8, CX)
+        inverse_x[1:, member, 8, member, :] = sine_x[7:-1:8]
+        inverse_x[:-1, member, 9, member, :] = sine_x[8::8]
+    along_y = np.kron(np.eye(CY // 2), steps)
+    spread = (sine_y @ along_y / 3.0).reshape(CY, NBY, 128).transpose(1, 0, 2)
+    spread = np.concatenate(split(spread), axis=2)
+    gather = (sine_y.reshape(CY, NBY, 64).transpose(1, 0, 2) @ np.kron(np.eye(32), steps)) / 6.0
+    gather = np.concatenate(split(gather), axis=2)
+    edge_y = np.zeros((NBY, 16, CY))
+    edge_y[1:, 0] = sine_y[63:-1:64]
+    edge_y[:-1, 1] = sine_y[64::64]
+    halo = np.zeros((96, 128))
+    for side in range(2):
+        halo[32 * side : 32 * side + 32, 16 * side : 16 * side + 16] = np.kron(np.eye(8), steps).T
+        halo[64 + 16 * side : 80 + 16 * side, 32 + 16 * side : 40 + 16 * side] = np.kron(np.eye(4), steps).T
+    halo = np.concatenate([halo, halo], axis=1)
+    plane_xz = np.kron(np.kron(np.eye(4), steps), np.kron(np.eye(8), steps))
     plane = (spectrum(CX)[:, None] + spectrum(CZ)[None, :]).astype(np.float32)
     return (
-        rounded(restrict_y),
         rounded(restrict_z),
         rounded(prolong_z),
-        rounded(sine_y).reshape(NBY, 64, CY),
+        gather,
         rounded(sine_z),
         rounded(forward_x.reshape(256, 256)),
-        rounded(inverse_x.reshape(NBX, 16, 256)),
+        rounded(inverse_x.reshape(NBX, 32, 256)),
         spread,
+        rounded(edge_y),
+        rounded(halo),
+        rounded(plane_xz),
         plane,
         spectrum(CY).astype(np.float32),
     )
@@ -82,23 +101,23 @@
 
 
 def kernel(
-    forcing_hbm, start_hbm, class_ref, coef, eigen_y, ry_hbm, rz_hbm, pz_hbm, sy_hbm, sz_hbm,
-    fx_hbm, ix_hbm, sp_hbm, plane_hbm,
+    forcing_hbm, start_hbm, class_ref, coef, eigen_y, rz_hbm, pz_hbm, gy_hbm, sz_hbm,
+    fx_hbm, ix_hbm, sp_hbm, ey_hbm, ph_hbm, kxz_hbm, plane_hbm,
     out_hbm, resid_hbm,
     f, s, z, r, inner, kap, beta, base, diag, dinv, wx, wxb, wzl, wzh, wzb, wyl, wyh, wyb,
-    xh, zh, yh, zsend, ysend, kx, kz, ky, kzsend, kysend,
-    ry, rz, pz, sy, sz, fx, ix, sp, plane, invlam, fine, swap,
-    c0, va, vsend, xg, vb, vbsend, c5, last,
-    load_sem, halo_s, halo_r, kap_s, kap_r, y1_s, y1_r, z1_s, z1_r, x_s, x_r, z2_s, z2_r, y2_s, y2_r,
+    xh, zh, yh, zsend, ysend, kx, kz, ky, kzsend, kysend, yadd,
+    rz, pz, gy, sz, fx, ix, sp, ey, ph, kxz, plane, invlam, fine, swap, wide_swap,
+    va, vsend, xg, vb, vbsend, last,
+    load_sem, halo_s, halo_r, kap_s, kap_r, z1_s, z1_r, x_s, x_r, z2_s, z2_r,
 ):
     ib, iy, iz = lax.axis_index("bx"), lax.axis_index("by"), lax.axis_index("bz")
     loads = [
         pltpu.make_async_copy(src, dst, load_sem.at[i])
         for i, (src, dst) in enumerate(
             [
-                (start_hbm, s.at[0]), (forcing_hbm, f), (ry_hbm, ry), (rz_hbm, rz), (pz_hbm, pz),
-                (sy_hbm.at[iy], sy), (sz_hbm, sz), (fx_hbm, fx), (ix_hbm.at[ib], ix),
-                (sp_hbm.at[iy], sp), (plane_hbm, plane),
+                (start_hbm, s.at[0]), (forcing_hbm, f), (plane_hbm, plane), (rz_hbm, rz), (pz_hbm, pz),
+                (gy_hbm.at[iy], gy), (sz_hbm, sz), (fx_hbm, fx), (ix_hbm.at[ib], ix),
+                (sp_hbm.at[iy], sp), (ey_hbm.at[iy], ey), (ph_hbm, ph), (kxz_hbm, kxz),
             ]
         )
     ]
@@ -108,21 +127,15 @@
     def x_peer(offset):
         return lax.rem(ib // 4 + offset[0], 4) * 4 + lax.rem(lax.rem(ib, 4) + offset[1], 4)
 
-    def z_peer(offset):
-        return lax.rem(iz + offset, NBZ)
-
-    def y_peer(offset):
-        return lax.rem(iy + offset, NBY)
-
-    z_order = (4, 3, 5, 2, 6, 1, 7)
-    y_order = (2, 3, 1)
+    def plane_peer(offset):
+        return lax.rem(iy + offset[0], NBY), lax.rem(iz + offset[1], NBZ)
+
     barrier = pltpu.get_barrier_semaphore()
     for offset in OFFSETS:
         pl.semaphore_signal(barrier, inc=1, device_id={"bx": x_peer(offset)}, device_id_type=MESH)
-    for offset in z_order:
-        pl.semaphore_signal(barrier, inc=1, device_id={"bz": z_peer(offset)}, device_id_type=MESH)
-    for offset in y_order:
-        pl.semaphore_signal(barrier, inc=1, device_id={"by": y_peer(offset)}, device_id_type=MESH)
+    for offset in PLANE:
+        py, pz_ = plane_peer(offset)
+        pl.semaphore_signal(barrier, inc=1, device_id={"by": py, "bz": pz_}, device_id_type=MESH)
 
     row = lax.broadcasted_iota(jnp.int32, (32, 128), 0)
     lane = lax.broadcasted_iota(jnp.int32, (32, 128), 1)
@@ -187,7 +200,7 @@
         remote(kysend, ky.at[1], kap_s.at[4], kap_r.at[4], {"by": ya}),
         remote(kysend, ky.at[0], kap_s.at[5], kap_r.at[5], {"by": yb}),
     ]
-    pl.semaphore_wait(barrier, len(OFFSETS) + len(z_order) + len(y_order))
+    pl.semaphore_wait(barrier, len(OFFSETS) + len(PLANE))
     for copy in kappa_copies:
         copy.start()
     copies = halo(s.at[0], 0, 0)
@@ -233,7 +246,7 @@
     for index in range(1, 16):
         kbar, sbar = kbar + coef[0, index], sbar + coef[1, index]
     kbar, sbar = kbar * 0.0625, sbar * 0.0625
-    loads[10].wait()
+    loads[2].wait()
     mode = iy * 64 + iz * 8
     for member in range(2):
         for pair in range(4):
@@ -277,21 +290,27 @@
         diag[x] = total
         dinv[x] = DAMPING / total
 
-    def outer_sum(slot):
-        inner[0] = inner[0] + wxb[0] * xh[slot, 0]
-        inner[15] = inner[15] + wxb[1] * xh[slot, 1]
-        low_y, high_y = jnp.transpose(yh[slot, 0]), jnp.transpose(yh[slot, 1])
+    def outer_sum(x_sides, z_sides, y_rows):
+        inner[0] = inner[0] + wxb[0] * x_sides[0]
+        inner[15] = inner[15] + wxb[1] * x_sides[1]
+        columns = jnp.transpose(y_rows)
         wide = lax.broadcasted_iota(jnp.int32, (128, 128), 1)
         for e in range(4):
-            low = jnp.broadcast_to(low_y[:, 2 * e : 2 * e + 1], (128, 128))
-            high = jnp.broadcast_to(high_y[:, 2 * e + 1 : 2 * e + 2], (128, 128))
+            low = jnp.broadcast_to(columns[:, e : e + 1], (128, 128))
+            high = jnp.broadcast_to(columns[:, 4 + e : 5 + e], (128, 128))
             other = jnp.where(wide == 0, low, high).reshape(4, 32, 128)
             weight = wyb[e]
             for j in range(4):
                 x = 4 * e + j
                 inner[x] = inner[x] + weight * other[j]
-                inner[x, 0:8, :] = inner[x, 0:8, :] + wzb[0, e] * zh[slot, 0, x : x + 1, :]
-                inner[x, 24:32, :] = inner[x, 24:32, :] + wzb[1, e] * zh[slot, 1, x : x + 1, :]
+                inner[x, 0:8, :] = inner[x, 0:8, :] + wzb[0, e] * z_sides[0][x : x + 1, :]
+                inner[x, 24:32, :] = inner[x, 24:32, :] + wzb[1, e] * z_sides[1][x : x + 1, :]
+
+    def arrived(slot):
+        for e in range(4):
+            yadd[e : e + 1, :] = yh[slot, 0, 2 * e : 2 * e + 1, :]
+            yadd[4 + e : 5 + e, :] = yh[slot, 1, 2 * e + 1 : 2 * e + 2, :]
+        return [xh[slot, 0], xh[slot, 1]], [zh[slot, 0], zh[slot, 1]], yadd[...]
 
     def residual(field, store):
         def step(e, carry):
@@ -309,16 +328,16 @@
 
     block = lax.broadcasted_iota(jnp.int32, (8, 128), 1) // 16
     loads[1].wait()
-    for load in loads[2:10]:
+    for load in loads[3:]:
         load.wait()
+    for copy in copies:
+        copy.wait()
+    outer_sum(*arrived(0))
+    residual(s.at[0], r)
+    lane8 = lax.broadcasted_iota(jnp.int32, (8, 128), 1)
+    me = iy * NBZ + iz
 
     for cycle in range(CYCLES):
-        for copy in copies:
-            copy.wait()
-        field = s.at[cycle]
-        outer_sum(2 * cycle)
-        residual(field, r)
-
         for e in range(4):
             one, two, three, four = (r[4 * e + j] for j in range(4))
             for half, value in ((0, 3.0 * one + 2.0 * two + three), (1, two + 2.0 * three + 3.0 * four)):
@@ -326,47 +345,39 @@
                 at = pl.ds((2 * e + half) * 32, 32)
                 fine[at, 0:128] = high
                 fine[at, 128:256] = (value - high.astype(F32)).astype(BF16)
-        value = lax.dot_general(ry[...], fine[...], (((1,), (1,)), ((), ())), preferred_element_type=F32)
-        high = value.astype(BF16)
-        low = (value - high.astype(F32)).astype(BF16)
-        value = jnp.dot(high, rz[...], preferred_element_type=F32) + jnp.dot(
-            low, rz[...], preferred_element_type=F32
-        )
-        c0[cycle, iy] = (value * (1.0 / 216.0)).astype(BF16)
-        sends = [
-            remote(c0.at[cycle, iy], c0.at[cycle, iy], y1_s.at[cycle, y_peer(o)], y1_r.at[cycle, iy], {"by": y_peer(o)})
-            for o in y_order
-        ]
-        for copy in sends:
+        value = jnp.dot(rz[...], fine[...], preferred_element_type=F32)
+        value = ((value[:, 0:128] + value[:, 128:256]) * (1.0 / 36.0)).astype(BF16)
+        value = jnp.concatenate([value, value], axis=1)
+        value = lax.dot_general(gy[...], value, (((1,), (1,)), ((), ())), preferred_element_type=F32)
+        vsend[cycle] = value.reshape(32, 8, 128).astype(BF16)
+
+        def forward(offset, receive=False):
+            py, pz_ = plane_peer(offset)
+            p = py * NBZ + pz_
+            here = p if receive else me
+            return remote(
+                vsend.at[cycle, p], va.at[cycle, here], z1_s.at[cycle, p], z1_r.at[cycle, here], {"by": py, "bz": pz_}
+            )
+
+        plane_sends = [forward(o) for o in PLANE]
+        for copy in plane_sends:
             copy.start()
+        va[cycle, me] = vsend[cycle, me]
 
         smooth = z.at[cycle]
         smooth[...] = r[...] * dinv[...]
         pack(smooth, 2 * cycle + 1)
         smooth_copies = halo(smooth, 2 * cycle + 1, 1)
-
-        for o in y_order:
-            p = y_peer(o)
-            remote(c0.at[cycle, p], c0.at[cycle, p], y1_s.at[cycle, p], y1_r.at[cycle, p], {"by": p}).wait_recv()
-        value = jnp.dot(sy[...], c0[cycle].reshape(CY, 128), preferred_element_type=F32)
-        vsend[cycle] = value.reshape(8, 8, 128).astype(BF16)
-        z_sends = [
-            remote(vsend.at[cycle, z_peer(o)], va.at[cycle, iz], z1_s.at[cycle, z_peer(o)], z1_r.at[cycle, iz], {"bz": z_peer(o)})
-            for o in z_order
-        ]
-        for copy in z_sends:
-            copy.start()
-        va[cycle, iz] = vsend[cycle, iz]
         for copy in smooth_copies:
             copy.start()
         inner_sum(smooth)
-        for copy in sends:
-            copy.wait_send()
-        for o in z_order:
-            p = z_peer(o)
-            remote(vsend.at[cycle, p], va.at[cycle, p], z1_s.at[cycle, p], z1_r.at[cycle, p], {"bz": p}).wait_recv()
-        parts = turn([va[cycle, i].astype(F32) for i in range(8)], block)
-        value = jnp.concatenate(parts, axis=0).astype(BF16)
+        for o in PLANE:
+            forward(o, True).wait_recv()
+        parts = []
+        for i in range(8):
+            one, two, three, four = (va[cycle, 8 * j + i].astype(F32) for j in range(4))
+            parts.append((one + two) + (three + four))
+        value = jnp.concatenate(turn(parts, block), axis=0).astype(BF16)
         swap[...] = jnp.dot(value, sz[...], preferred_element_type=F32)
         value = jnp.concatenate([swap[pl.ds(m, 8, stride=8), :] for m in range(8)], axis=0)
         xg[cycle, ib] = value.reshape(4, 16, 128).astype(BF16)
@@ -376,13 +387,18 @@
         ]
         for copy in x_sends:
             copy.start()
-        for copy in z_sends:
+        for copy in plane_sends:
             copy.wait_send()
 
+        after = s.at[cycle + 1]
         for copy in smooth_copies:
             copy.wait()
-        outer_sum(2 * cycle + 1)
-        s[cycle + 1] = s[cycle] + ((2.0 - DAMPING) * smooth[...] + dinv[...] * inner[...])
+        outer_sum(*arrived(2 * cycle + 1))
+        after[...] = s[cycle] + ((2.0 - DAMPING) * smooth[...] + dinv[...] * inner[...])
+        pack(after, 2 * cycle + 2)
+        copies = halo(after, 2 * cycle + 2, 0)
+        for copy in copies:
+            copy.start()
 
         for o in OFFSETS:
             p = x_peer(o)
@@ -397,64 +413,75 @@
             value = jnp.dot(ix[...], value, preferred_element_type=F32)
             parts += [value[:, 0:128], value[:, 128:256]]
         value = jnp.concatenate(parts, axis=0).astype(BF16)
-        swap[...] = jnp.dot(value, sz[...], preferred_element_type=F32)
-        parts = turn([swap[pl.ds(i, 8, stride=8), :] for i in range(8)], block)
+        wide_swap[...] = jnp.dot(value, sz[...], preferred_element_type=F32)
+        lines = [wide_swap[pl.ds(i, 8, stride=16), :] for i in range(10)]
+        low = high = none = jnp.zeros((8, 128), F32)
         for i in range(8):
-            vbsend[cycle, i] = parts[i].astype(BF16)
-        z_sends = [
-            remote(vbsend.at[cycle, z_peer(o)], vb.at[cycle, iz], z2_s.at[cycle, z_peer(o)], z2_r.at[cycle, iz], {"bz": z_peer(o)})
-            for o in z_order
-        ]
-        for copy in z_sends:
+            low = jnp.where(lane8 % 16 == i, pltpu.roll(lines[i], 1 + i, 1), low)
+            high = jnp.where(lane8 % 16 == i, pltpu.roll(lines[i], 112 + i, 1), high)
+        own = turn(lines[0:8], block)
+        beyond = turn([lines[8], lines[9], low, high, none, none, none, none], block)
+        for i in range(8):
+            vbsend[cycle, i, 0] = own[i].astype(BF16)
+            vbsend[cycle, i, 1] = beyond[i].astype(BF16)
+
+        def backward(offset, receive=False):
+            py, pz_ = plane_peer(offset)
+            p = py * NBZ + pz_
+            here = p if receive else me
+            return remote(
+                vbsend.at[cycle, pz_], vb.at[cycle, here], z2_s.at[cycle, p], z2_r.at[cycle, here], {"by": py, "bz": pz_}
+            )
+
+        plane_sends = [backward(o) for o in PLANE]
+        for copy in plane_sends:
             copy.start()
-        vb[cycle, iz] = vbsend[cycle, iz]
+        vb[cycle, me] = vbsend[cycle, iz]
         for copy in x_sends:
             copy.wait_send()
-        for o in z_order:
-            p = z_peer(o)
-            remote(vbsend.at[cycle, p], vb.at[cycle, p], z2_s.at[cycle, p], z2_r.at[cycle, p], {"bz": p}).wait_recv()
-        c5[cycle, iy] = vb[cycle].astype(F32).reshape(64, 128).astype(BF16)
-        sends = [
-            remote(c5.at[cycle, iy], c5.at[cycle, iy], y2_s.at[cycle, y_peer(o)], y2_r.at[cycle, iy], {"by": y_peer(o)})
-            for o in y_order
-        ]
-        for copy in sends:
-            copy.start()
-        for copy in z_sends:
-            copy.wait_send()
-        for o in y_order:
-            p = y_peer(o)
-            remote(c5.at[cycle, p], c5.at[cycle, p], y2_s.at[cycle, p], y2_r.at[cycle, p], {"by": p}).wait_recv()
-
-        modes = c5[cycle].reshape(CY, 128)
-        over = (((0,), (0,)), ((), ()))
-        value = lax.dot_general(modes, sp[0], over, preferred_element_type=F32) + lax.dot_general(
-            modes, sp[1], over, preferred_element_type=F32
+        for copy in copies:
+            copy.wait()
+        x_sides, z_sides, y_rows = arrived(2 * cycle + 2)
+        for o in PLANE:
+            backward(o, True).wait_recv()
+
+        own = vb[cycle, :, 0].astype(F32).reshape(CY, 128).astype(BF16)
+        beyond = vb[cycle, :, 1].astype(F32).reshape(CY, 128).astype(BF16)
+        value = lax.dot_general(
+            jnp.concatenate([own, beyond], axis=1), sp[...], (((0,), (0,)), ((), ())), preferred_element_type=F32
         )
+        value = value[:, 0:128] + value[:, 128:256]
         high = value.astype(BF16)
         low = (value - high.astype(F32)).astype(BF16)
-        value = jnp.dot(pz[...], jnp.concatenate([high, low], axis=0), preferred_element_type=F32)
+        value = jnp.dot(pz[...], jnp.concatenate([high[0:128], low[0:128]], axis=0), preferred_element_type=F32)
         value = (value * (1.0 / 3.0)).reshape(8, 32, 128)
-        after = s.at[cycle + 1]
+        outside = jnp.dot(ph[...], jnp.concatenate([high[128:256], low[128:256]], axis=0), preferred_element_type=F32)
+        outside = outside * (1.0 / 3.0)
+        edge = jnp.dot(ey[...], own, preferred_element_type=F32)
+        high = edge.astype(BF16)
+        low = (edge - high.astype(F32)).astype(BF16)
+        edge = jnp.dot(jnp.concatenate([high, low], axis=0), kxz[...], preferred_element_type=F32)
+        edge = (edge[0:8] + edge[16:24]) * (1.0 / 9.0)
         for e in range(4):
             one, two = value[2 * e], value[2 * e + 1]
             mixed = (one, one * (2.0 / 3.0) + two * (1.0 / 3.0), one * (1.0 / 3.0) + two * (2.0 / 3.0), two)
             for j in range(4):
                 after[4 * e + j] = after[4 * e + j] + mixed[j]
-        pack(after, 2 * cycle + 2)
-        copies = halo(after, 2 * cycle + 2, 0)
-        for copy in copies:
-            copy.start()
-        for copy in sends:
+            yadd[e : e + 1, :] = edge[0:1, 128 * e : 128 * e + 128]
+            yadd[4 + e : 5 + e, :] = edge[1:2, 128 * e : 128 * e + 128]
+        if cycle == CYCLES - 1:
+            store = pltpu.make_async_copy(s.at[CYCLES], out_hbm, load_sem.at[0])
+            store.start()
+        for copy in plane_sends:
             copy.wait_send()
         inner_sum(after)
-
-    store = pltpu.make_async_copy(s.at[CYCLES], out_hbm, load_sem.at[0])
-    store.start()
-    for copy in copies:
-        copy.wait()
-    outer_sum(2 * CYCLES)
-    residual(s.at[CYCLES], last)
+        outer_sum(
+            [x_sides[0] + outside[0:32], x_sides[1] + outside[32:64]],
+            [z_sides[0] + outside[64:80], z_sides[1] + outside[80:96]],
+            y_rows + yadd[...],
+        )
+        residual(after, last if cycle == CYCLES - 1 else r)
+
     final = pltpu.make_async_copy(last, resid_hbm, load_sem.at[1])
     final.start()
     store.wait()
@@ -478,19 +505,17 @@
         + [vmem((5, 2, 32, 128), F32), vmem((5, 2, 16, 128), F32), vmem((5, 2, 8, 128), F32)]
         + [vmem((5, 2, 16, 128), F32), vmem((5, 8, 128), F32)]
         + [vmem((2, 32, 128), F32), vmem((2, 8, 128), F32), vmem((2, 8, 128), F32)]
-        + [vmem((8, 128), F32), vmem((8, 128), F32)]
-        + [vmem((64, 256), BF16), vmem((256, 128), BF16), vmem((256, 256), BF16), vmem((64, 256), BF16)]
-        + [vmem((128, 128), BF16), vmem((256, 256), BF16), vmem((16, 256), BF16), vmem((2, 256, 128), BF16)]
-        + [vmem((128, 128), F32), vmem((256, 512), F32), vmem((256, 256), BF16), vmem((64, 128), F32)]
-        + [vmem((2, 4, 64, 128), BF16), vmem((2, 8, 8, 128), BF16), vmem((2, 8, 8, 128), BF16)]
-        + [vmem((2, 16, 4, 16, 128), BF16), vmem((2, 8, 8, 128), BF16), vmem((2, 8, 8, 128), BF16)]
-        + [vmem((2, 4, 64, 128), BF16), vmem(full, F32)]
-        + [dma((11,)), dma((2, 6)), dma((2, 6)), dma((6,)), dma((6,))]
-        + [dma((2, 4))] * 2
-        + [dma((2, 8))] * 2
+        + [vmem((8, 128), F32)] * 3
+        + [vmem((128, 256), BF16), vmem((256, 256), BF16), vmem((256, 256), BF16), vmem((128, 128), BF16)]
+        + [vmem((256, 256), BF16), vmem((32, 256), BF16), vmem((256, 256), BF16), vmem((16, 256), BF16)]
+        + [vmem((96, 256), BF16), vmem((128, 512), BF16), vmem((128, 128), F32), vmem((256, 512), F32)]
+        + [vmem((256, 256), BF16), vmem((64, 128), F32), vmem((128, 128), F32)]
+        + [vmem((2, 32, 8, 128), BF16), vmem((2, 32, 8, 128), BF16), vmem((2, 16, 4, 16, 128), BF16)]
+        + [vmem((2, 32, 2, 8, 128), BF16), vmem((2, 8, 2, 8, 128), BF16), vmem(full, F32)]
+        + [dma((13,)), dma((2, 6)), dma((2, 6)), dma((6,)), dma((6,))]
+        + [dma((2, 32))] * 2
         + [dma((2, 16))] * 2
-        + [dma((2, 8))] * 2
-        + [dma((2, 4))] * 2
+        + [dma((2, 32))] * 2
     )
     anywhere = pl.BlockSpec(memory_space=pl.ANY)
     scalar = pl.BlockSpec(memory_space=pltpu.SMEM)
@@ -498,7 +523,7 @@
     return pl.pallas_call(
         kernel,
         out_shape=(shape, shape),
-        in_specs=[anywhere, anywhere, pl.BlockSpec(memory_space=pltpu.VMEM), scalar, scalar] + [anywhere] * 9,
+        in_specs=[anywhere, anywhere, pl.BlockSpec(memory_space=pltpu.VMEM), scalar, scalar] + [anywhere] * 11,
         out_specs=(anywhere, anywhere),
         scratch_shapes=scratch,
         compiler_params=pltpu.CompilerParams(collective_id=0, has_side_effects=True),

time: 86.8 us -> 75.9 us (0.87)
  Pallas kernels: 83.6 us -> 72.6 us
    pallas_call x1, Pallas kernels: 83.6 us -> 72.6 us  [body(): pl.pallas_call(kernel, out_shape=(shape, shape), in_specs=[anywhere, anyw...]
where the time goes in v2:
time: 75.9 us; the launch traced here: 75.7 us
  Pallas kernels  72.6 us (96%)
  local copies, waits for them, and re-layouts  2.42 us (3%)
    pallas_call x1, Pallas kernels, body(): pl.pallas_call(kernel, out_shape=(shape, shape), in_specs=[anywhere, anyw...  72.6 us
    unnamed x4, local copies, waits for them, and re-layouts  2.42 us

profile of v2, /device:TPU:1, one launch (start us, length us, event | category | flops | bytes accessed | tf_op | source)
XLA Modules:
  0.0 75.7 jit_solution(8037711472963300976)
XLA Ops:
  0.6 72.6 %cycles.1 = (f32[16,32,128]{2,1,0:T(8,128)}, f32[16,32,128]{2,1,0:T(8,128)}) custom-call(f32[16,32,128]{2,1,0:T(8,128)} %forcing_hbm.1, f32[16,32,128]{2,1,0:T(8,128)} %start_hbm.1, s32[32,32]{1,0:T(8,128)} %bitcast.1, f32[3,16]{1,0:T(4,128)} %coef.1, f32[256]{0:T(256)} %constant.35.clone.eigen_y, bf16[128,256]{1,0:T(8,128)(2,1)} %constant.24.clone.rz_hbm, ...), custom_call_target="tpu_custom_call" | custom-call | tf_op jit(solution)/shard_map/cycles/pallas_call | solution.py:523
  73.2 0.0 copy-start
  73.2 1.7 %copy.20 = f32[16,32,128]{2,1,0:T(8,128)} copy(f32[16,32,128]{2,1,0:T(8,128)} %get-tuple-element.4) | data formatting | bytes 524288
  74.9 0.0 copy-done
  74.9 0.7 copy.21
Async XLA Ops:
  73.2 1.7 %copy-start = (f32[16,32,128]{2,1,0:T(8,128)S(1)}, f32[16,32,128]{2,1,0:T(8,128)}, u32[]{:S(2)}) copy-start(f32[16,32,128]{2,1,0:T(8,128)} %get-tuple-element.5) | copy-start | bytes 786436

commit v3 on v2

--- a/solution.py
+++ b/solution.py
@@ -21,6 +21,12 @@
 
 
 PLANE = [(a, b) for b in (4, 3, 5, 2, 6, 1, 7, 0) for a in (2, 3, 1, 0) if (a, b) != (0, 0)]
+
+
+ROWS = {
+    "rz": slice(0, 128), "pz": slice(128, 384), "fx": slice(384, 640),
+    "ph": slice(640, 736), "kxz": slice(736, 992), "sz": slice(992, 1120),
+}
 
 
 def rounded(value):
@@ -70,17 +76,15 @@
     halo = np.concatenate([halo, halo], axis=1)
     plane_xz = np.kron(np.kron(np.eye(4), steps), np.kron(np.eye(8), steps))
     plane = (spectrum(CX)[:, None] + spectrum(CZ)[None, :]).astype(np.float32)
+    common = np.zeros((1120, 256))
+    for name, value in (("rz", restrict_z), ("pz", prolong_z), ("fx", forward_x.reshape(256, 256)), ("ph", halo), ("sz", sine_z)):
+        common[ROWS[name], : value.shape[1]] = value
+    common[ROWS["kxz"]] = plane_xz.reshape(128, 2, 256).transpose(1, 0, 2).reshape(256, 256)
+    along = np.concatenate([np.asarray(v, np.float64) for v in (gather, spread, edge_y)], axis=1)
     return (
-        rounded(restrict_z),
-        rounded(prolong_z),
-        gather,
-        rounded(sine_z),
-        rounded(forward_x.reshape(256, 256)),
+        rounded(common),
+        rounded(along),
         rounded(inverse_x.reshape(NBX, 32, 256)),
-        spread,
-        rounded(edge_y),
-        rounded(halo),
-        rounded(plane_xz),
         plane,
         spectrum(CY).astype(np.float32),
     )
@@ -101,13 +105,12 @@
 
 
 def kernel(
-    forcing_hbm, start_hbm, class_ref, coef, eigen_y, rz_hbm, pz_hbm, gy_hbm, sz_hbm,
-    fx_hbm, ix_hbm, sp_hbm, ey_hbm, ph_hbm, kxz_hbm, plane_hbm,
-    out_hbm, resid_hbm,
+    forcing_hbm, start_hbm, class_ref, coef, eigen_y, common_hbm, along_hbm, ix_hbm, plane_hbm,
+    out_ref, resid_ref,
     f, s, z, r, inner, kap, beta, base, diag, dinv, wx, wxb, wzl, wzh, wzb, wyl, wyh, wyb,
-    xh, zh, yh, zsend, ysend, kx, kz, ky, kzsend, kysend, yadd,
-    rz, pz, gy, sz, fx, ix, sp, ey, ph, kxz, plane, invlam, fine, swap, wide_swap,
-    va, vsend, xg, vb, vbsend, last,
+    halos, zsend, ysend, khalo, kzsend, kysend, yadd,
+    common, along, ix, plane, invlam, fine, swap, wide_swap,
+    va, vsend, xg, vb, vbsend,
     load_sem, halo_s, halo_r, kap_s, kap_r, z1_s, z1_r, x_s, x_r, z2_s, z2_r,
 ):
     ib, iy, iz = lax.axis_index("bx"), lax.axis_index("by"), lax.axis_index("bz")
@@ -115,9 +118,8 @@
         pltpu.make_async_copy(src, dst, load_sem.at[i])
         for i, (src, dst) in enumerate(
             [
-                (start_hbm, s.at[0]), (forcing_hbm, f), (plane_hbm, plane), (rz_hbm, rz), (pz_hbm, pz),
-                (gy_hbm.at[iy], gy), (sz_hbm, sz), (fx_hbm, fx), (ix_hbm.at[ib], ix),
-                (sp_hbm.at[iy], sp), (ey_hbm.at[iy], ey), (ph_hbm, ph), (kxz_hbm, kxz),
+                (start_hbm, s.at[0]), (forcing_hbm, f), (plane_hbm, plane),
+                (common_hbm, common), (along_hbm.at[iy], along), (ix_hbm.at[ib], ix),
             ]
         )
     ]
@@ -133,7 +135,7 @@
     barrier = pltpu.get_barrier_semaphore()
     for offset in OFFSETS:
         pl.semaphore_signal(barrier, inc=1, device_id={"bx": x_peer(offset)}, device_id_type=MESH)
-    for offset in PLANE:
+    for offset in PLANE[::-1]:
         py, pz_ = plane_peer(offset)
         pl.semaphore_signal(barrier, inc=1, device_id={"by": py, "bz": pz_}, device_id_type=MESH)
 
@@ -179,32 +181,34 @@
             src_ref=src, dst_ref=dst, send_sem=send, recv_sem=recv, device_id=device, device_id_type=MESH
         )
 
-    def halo(field, slot, kind):
-        ss, rs = halo_s.at[kind], halo_r.at[kind]
+    def halo(field, slot):
+        to, ss, rs = halos.at[slot], halo_s.at[slot], halo_r.at[slot]
         return [
-            remote(field.at[0], xh.at[slot, 1], ss.at[0], rs.at[0], {"bx": xa}),
-            remote(field.at[15], xh.at[slot, 0], ss.at[1], rs.at[1], {"bx": xb}),
-            remote(zsend.at[slot, 0], zh.at[slot, 1], ss.at[2], rs.at[2], {"bz": za}),
-            remote(zsend.at[slot, 1], zh.at[slot, 0], ss.at[3], rs.at[3], {"bz": zb}),
-            remote(ysend.at[slot], yh.at[slot, 1], ss.at[4], rs.at[4], {"by": ya}),
-            remote(ysend.at[slot], yh.at[slot, 0], ss.at[5], rs.at[5], {"by": yb}),
+            remote(field.at[0], to.at[32:64], ss, rs, {"bx": xa}),
+            remote(field.at[15], to.at[0:32], ss, rs, {"bx": xb}),
+            remote(zsend.at[slot, 0], to.at[80:96], ss, rs, {"bz": za}),
+            remote(zsend.at[slot, 1], to.at[64:80], ss, rs, {"bz": zb}),
+            remote(ysend.at[slot], to.at[104:112], ss, rs, {"by": ya}),
+            remote(ysend.at[slot], to.at[96:104], ss, rs, {"by": yb}),
         ]
+
+    def halo_wait(slot):
+        remote(halos.at[slot], halos.at[slot], halo_s.at[slot], halo_r.at[slot], {"bx": xa}).wait()
 
     loads[0].wait()
     pack(s.at[0], 0)
     kappa_copies = [
-        remote(kap.at[0], kx.at[1], kap_s.at[0], kap_r.at[0], {"bx": xa}),
-        remote(kap.at[3], kx.at[0], kap_s.at[1], kap_r.at[1], {"bx": xb}),
-        remote(kzsend, kz.at[1], kap_s.at[2], kap_r.at[2], {"bz": za}),
-        remote(kzsend, kz.at[0], kap_s.at[3], kap_r.at[3], {"bz": zb}),
-        remote(kysend, ky.at[1], kap_s.at[4], kap_r.at[4], {"by": ya}),
-        remote(kysend, ky.at[0], kap_s.at[5], kap_r.at[5], {"by": yb}),
+        remote(kap.at[0], khalo.at[32:64], kap_s.at[0], kap_r.at[0], {"bx": xa}),
+        remote(kap.at[3], khalo.at[0:32], kap_s.at[0], kap_r.at[0], {"bx": xb}),
+        remote(kzsend, khalo.at[72:80], kap_s.at[0], kap_r.at[0], {"bz": za}),
+        remote(kzsend, khalo.at[64:72], kap_s.at[0], kap_r.at[0], {"bz": zb}),
+        remote(kysend, khalo.at[88:96], kap_s.at[0], kap_r.at[0], {"by": ya}),
+        remote(kysend, khalo.at[80:88], kap_s.at[0], kap_r.at[0], {"by": yb}),
     ]
     pl.semaphore_wait(barrier, len(OFFSETS) + len(PLANE))
     for copy in kappa_copies:
         copy.start()
-    copies = halo(s.at[0], 0, 0)
-    for copy in copies:
+    for copy in halo(s.at[0], 0):
         copy.start()
 
     zero = jnp.zeros((32, 128), F32)
@@ -259,16 +263,15 @@
     x_in = (inside(ib > 0), inside(ib < NBX - 1))
     z_in = (inside(iz > 0), inside(iz < NBZ - 1))
     y_in = (inside(iy > 0), inside(iy < NBY - 1))
-    for copy in kappa_copies:
-        copy.wait()
+    remote(khalo, khalo, kap_s.at[0], kap_r.at[0], {"bx": xa}).wait()
     row8 = lax.broadcasted_iota(jnp.int32, (8, 128), 0)
     ends = []
     for side, e in ((0, 0), (1, 3)):
-        weight = kap[e] + kx[side] * x_in[side]
+        weight = kap[e] + khalo[32 * side : 32 * side + 32] * x_in[side]
         wxb[side] = weight * x_in[side]
         ends.append(weight)
-    low_y = jnp.transpose(ky[0])[:, 0:1]
-    high_y = jnp.transpose(ky[1])[:, 1:2]
+    low_y = jnp.transpose(khalo[80:88])[:, 0:1]
+    high_y = jnp.transpose(khalo[88:96])[:, 1:2]
     wide = lax.broadcasted_iota(jnp.int32, (128, 128), 1)
     outer = jnp.where(wide == 0, y_in[0], jnp.where(wide == 127, y_in[1], 0.0))
     other = jnp.where(wide == 0, jnp.broadcast_to(low_y, (128, 128)), jnp.broadcast_to(high_y, (128, 128)))
@@ -277,8 +280,8 @@
     wyb[...] = (edge_y * outer).reshape(4, 32, 128)
     base[...] = base[...] + edge_y.reshape(4, 32, 128)
     for e in range(4):
-        low = jnp.where(row8 == 0, kap[e, 0:8, :] + kz[0, 4 + e : 5 + e, :] * z_in[0], 0.0)
-        high = jnp.where(row8 == 7, kap[e, 24:32, :] + kz[1, e : e + 1, :] * z_in[1], 0.0)
+        low = jnp.where(row8 == 0, kap[e, 0:8, :] + khalo[68 + e : 69 + e, :] * z_in[0], 0.0)
+        high = jnp.where(row8 == 7, kap[e, 24:32, :] + khalo[72 + e : 73 + e, :] * z_in[1], 0.0)
         wzb[0, e] = low * z_in[0]
         wzb[1, e] = high * z_in[1]
         base[e, 0:8, :] = base[e, 0:8, :] + low
@@ -288,7 +291,6 @@
         above = ends[1] if x == 15 else wx[x + 1]
         total = base[x // 4] + (below + above)
         diag[x] = total
-        dinv[x] = DAMPING / total
 
     def outer_sum(x_sides, z_sides, y_rows):
         inner[0] = inner[0] + wxb[0] * x_sides[0]
@@ -308,12 +310,46 @@
 
     def arrived(slot):
         for e in range(4):
-            yadd[e : e + 1, :] = yh[slot, 0, 2 * e : 2 * e + 1, :]
-            yadd[4 + e : 5 + e, :] = yh[slot, 1, 2 * e + 1 : 2 * e + 2, :]
-        return [xh[slot, 0], xh[slot, 1]], [zh[slot, 0], zh[slot, 1]], yadd[...]
+            yadd[slot, e : e + 1, :] = halos[slot, 96 + 2 * e : 97 + 2 * e, :]
+            yadd[slot, 4 + e : 5 + e, :] = halos[slot, 105 + 2 * e : 106 + 2 * e, :]
+        got = halos[slot, 0:96, :]
+        return [got[0:32], got[32:64]], [got[64:80], got[80:96]], yadd[slot]
+
+    def restricted(e, planes):
+        one, two, three, four = planes
+        for half, value in ((0, 3.0 * one + 2.0 * two + three), (1, two + 2.0 * three + 3.0 * four)):
+            high = value.astype(BF16)
+            at = pl.ds((2 * e + half) * 32, 32)
+            fine[at, 0:128] = high
+            fine[at, 128:256] = (value - high.astype(F32)).astype(BF16)
+
+    def fused(field, store, x_sides, z_sides, y_rows, last):
+        columns = jnp.transpose(y_rows)
+        wide = lax.broadcasted_iota(jnp.int32, (128, 128), 1)
+        for e in range(4):
+            low = jnp.broadcast_to(columns[:, e : e + 1], (128, 128))
+            high = jnp.broadcast_to(columns[:, 4 + e : 5 + e], (128, 128))
+            other = jnp.where(wide == 0, low, high).reshape(4, 32, 128)
+            planes = []
+            for j in range(4):
+                x = 4 * e + j
+                v = field[x]
+                total = wzl[e] * pltpu.roll(v, 1, 0) + wzh[e] * pltpu.roll(v, 31, 0)
+                total = total + wyl[e] * pltpu.roll(v, 1, 1) + wyh[e] * pltpu.roll(v, 127, 1)
+                total = total + wyb[e] * other[j]
+                total = total + (wxb[0] * x_sides[0] if x == 0 else wx[x] * field[x - 1])
+                total = total + (wxb[1] * x_sides[1] if x == 15 else wx[x + 1] * field[x + 1])
+                low_z = total[0:8] + wzb[0, e] * z_sides[0][x : x + 1, :]
+                high_z = total[24:32] + wzb[1, e] * z_sides[1][x : x + 1, :]
+                total = jnp.concatenate([low_z, total[8:24], high_z], axis=0)
+                value = (f[x] - (diag[x] * v - total)) - beta[e] * v * v * v
+                store[x] = value
+                planes.append(value)
+            if not last:
+                restricted(e, planes)
 
     def residual(field, store):
-        def step(e, carry):
+        for e in range(4):
             cube = beta[e]
             planes = []
             for j in range(4):
@@ -322,57 +358,50 @@
                 value = (f[x] - (diag[x] * v - inner[x])) - cube * v * v * v
                 store[x] = value
                 planes.append(value)
-            return carry
-
-        lax.fori_loop(0, 4, step, 0)
+            restricted(e, planes)
 
     block = lax.broadcasted_iota(jnp.int32, (8, 128), 1) // 16
     loads[1].wait()
     for load in loads[3:]:
         load.wait()
-    for copy in copies:
-        copy.wait()
+    halo_wait(0)
     outer_sum(*arrived(0))
     residual(s.at[0], r)
+    rz, pz, fx, ph = (common.at[ROWS[name]] for name in ("rz", "pz", "fx", "ph"))
+    sz = common.at[ROWS["sz"], 0:128]
+    kxz = common.at[ROWS["kxz"]]
+    gy, sp, ey = along.at[0:256], along.at[256:512], along.at[512:528]
     lane8 = lax.broadcasted_iota(jnp.int32, (8, 128), 1)
     me = iy * NBZ + iz
 
     for cycle in range(CYCLES):
-        for e in range(4):
-            one, two, three, four = (r[4 * e + j] for j in range(4))
-            for half, value in ((0, 3.0 * one + 2.0 * two + three), (1, two + 2.0 * three + 3.0 * four)):
-                high = value.astype(BF16)
-                at = pl.ds((2 * e + half) * 32, 32)
-                fine[at, 0:128] = high
-                fine[at, 128:256] = (value - high.astype(F32)).astype(BF16)
         value = jnp.dot(rz[...], fine[...], preferred_element_type=F32)
         value = ((value[:, 0:128] + value[:, 128:256]) * (1.0 / 36.0)).astype(BF16)
         value = jnp.concatenate([value, value], axis=1)
         value = lax.dot_general(gy[...], value, (((1,), (1,)), ((), ())), preferred_element_type=F32)
         vsend[cycle] = value.reshape(32, 8, 128).astype(BF16)
 
-        def forward(offset, receive=False):
+        def forward(offset):
             py, pz_ = plane_peer(offset)
-            p = py * NBZ + pz_
-            here = p if receive else me
             return remote(
-                vsend.at[cycle, p], va.at[cycle, here], z1_s.at[cycle, p], z1_r.at[cycle, here], {"by": py, "bz": pz_}
+                vsend.at[cycle, py * NBZ + pz_], va.at[cycle, me], z1_s.at[cycle], z1_r.at[cycle], {"by": py, "bz": pz_}
             )
 
-        plane_sends = [forward(o) for o in PLANE]
-        for copy in plane_sends:
-            copy.start()
+        for o in PLANE:
+            forward(o).start()
         va[cycle, me] = vsend[cycle, me]
 
         smooth = z.at[cycle]
+        if cycle == 0:
+            dinv[...] = DAMPING / diag[...]
         smooth[...] = r[...] * dinv[...]
         pack(smooth, 2 * cycle + 1)
-        smooth_copies = halo(smooth, 2 * cycle + 1, 1)
-        for copy in smooth_copies:
+        for copy in halo(smooth, 2 * cycle + 1):
             copy.start()
         inner_sum(smooth)
-        for o in PLANE:
-            forward(o, True).wait_recv()
+        some = va.at[cycle, pl.ds(0, 31)]
+        forward_all = remote(some, some, z1_s.at[cycle], z1_r.at[cycle], {"bz": zb})
+        forward_all.wait_recv()
         parts = []
         for i in range(8):
             one, two, three, four = (va[cycle, 8 * j + i].astype(F32) for j in range(4))
@@ -381,28 +410,21 @@
         swap[...] = jnp.dot(value, sz[...], preferred_element_type=F32)
         value = jnp.concatenate([swap[pl.ds(m, 8, stride=8), :] for m in range(8)], axis=0)
         xg[cycle, ib] = value.reshape(4, 16, 128).astype(BF16)
-        x_sends = [
-            remote(xg.at[cycle, ib], xg.at[cycle, ib], x_s.at[cycle, x_peer(o)], x_r.at[cycle, ib], {"bx": x_peer(o)})
-            for o in OFFSETS
-        ]
-        for copy in x_sends:
-            copy.start()
-        for copy in plane_sends:
-            copy.wait_send()
-
-        after = s.at[cycle + 1]
-        for copy in smooth_copies:
-            copy.wait()
+        for o in OFFSETS:
+            remote(xg.at[cycle, ib], xg.at[cycle, ib], x_s.at[cycle], x_r.at[cycle], {"bx": x_peer(o)}).start()
+        forward_all.wait_send()
+
+        final = cycle == CYCLES - 1
+        after = out_ref if final else s.at[cycle + 1]
+        halo_wait(2 * cycle + 1)
         outer_sum(*arrived(2 * cycle + 1))
         after[...] = s[cycle] + ((2.0 - DAMPING) * smooth[...] + dinv[...] * inner[...])
         pack(after, 2 * cycle + 2)
-        copies = halo(after, 2 * cycle + 2, 0)
-        for copy in copies:
+        for copy in halo(after, 2 * cycle + 2):
             copy.start()
-
-        for o in OFFSETS:
-            p = x_peer(o)
-            remote(xg.at[cycle, p], xg.at[cycle, p], x_s.at[cycle, p], x_r.at[cycle, p], {"bx": p}).wait_recv()
+        some = xg.at[cycle, pl.ds(0, 15)]
+        x_all = remote(some, some, x_s.at[cycle], x_r.at[cycle], {"bx": xa})
+        x_all.wait_recv()
         parts = []
         for half in range(2):
             value = jnp.concatenate(
@@ -425,25 +447,21 @@
             vbsend[cycle, i, 0] = own[i].astype(BF16)
             vbsend[cycle, i, 1] = beyond[i].astype(BF16)
 
-        def backward(offset, receive=False):
+        def backward(offset):
             py, pz_ = plane_peer(offset)
-            p = py * NBZ + pz_
-            here = p if receive else me
             return remote(
-                vbsend.at[cycle, pz_], vb.at[cycle, here], z2_s.at[cycle, p], z2_r.at[cycle, here], {"by": py, "bz": pz_}
+                vbsend.at[cycle, pz_], vb.at[cycle, me], z2_s.at[cycle], z2_r.at[cycle], {"by": py, "bz": pz_}
             )
 
-        plane_sends = [backward(o) for o in PLANE]
-        for copy in plane_sends:
-            copy.start()
+        for o in PLANE:
+            backward(o).start()
         vb[cycle, me] = vbsend[cycle, iz]
-        for copy in x_sends:
-            copy.wait_send()
-        for copy in copies:
-            copy.wait()
+        x_all.wait_send()
+        halo_wait(2 * cycle + 2)
         x_sides, z_sides, y_rows = arrived(2 * cycle + 2)
-        for o in PLANE:
-            backward(o, True).wait_recv()
+        some = vb.at[cycle, pl.ds(0, 31)]
+        back_all = remote(some, some, z2_s.at[cycle], z2_r.at[cycle], {"bz": zb})
+        back_all.wait_recv()
 
         own = vb[cycle, :, 0].astype(F32).reshape(CY, 128).astype(BF16)
         beyond = vb[cycle, :, 1].astype(F32).reshape(CY, 128).astype(BF16)
@@ -460,32 +478,26 @@
         edge = jnp.dot(ey[...], own, preferred_element_type=F32)
         high = edge.astype(BF16)
         low = (edge - high.astype(F32)).astype(BF16)
-        edge = jnp.dot(jnp.concatenate([high, low], axis=0), kxz[...], preferred_element_type=F32)
-        edge = (edge[0:8] + edge[16:24]) * (1.0 / 9.0)
+        edge = jnp.concatenate([high, low], axis=0)
+        edge = [jnp.dot(edge, kxz[128 * i : 128 * i + 128, :], preferred_element_type=F32) for i in range(2)]
+        edge = [(part[0:8] + part[16:24]) * (1.0 / 9.0) for part in edge]
         for e in range(4):
             one, two = value[2 * e], value[2 * e + 1]
             mixed = (one, one * (2.0 / 3.0) + two * (1.0 / 3.0), one * (1.0 / 3.0) + two * (2.0 / 3.0), two)
             for j in range(4):
                 after[4 * e + j] = after[4 * e + j] + mixed[j]
-            yadd[e : e + 1, :] = edge[0:1, 128 * e : 128 * e + 128]
-            yadd[4 + e : 5 + e, :] = edge[1:2, 128 * e : 128 * e + 128]
-        if cycle == CYCLES - 1:
-            store = pltpu.make_async_copy(s.at[CYCLES], out_hbm, load_sem.at[0])
-            store.start()
-        for copy in plane_sends:
-            copy.wait_send()
-        inner_sum(after)
-        outer_sum(
+            part = edge[e // 2][:, 128 * (e % 2) : 128 * (e % 2) + 128]
+            yadd[5, e : e + 1, :] = part[0:1]
+            yadd[5, 4 + e : 5 + e, :] = part[1:2]
+        fused(
+            after,
+            resid_ref if final else r,
             [x_sides[0] + outside[0:32], x_sides[1] + outside[32:64]],
             [z_sides[0] + outside[64:80], z_sides[1] + outside[80:96]],
-            y_rows + yadd[...],
+            y_rows + yadd[5],
+            final,
         )
-        residual(after, last if cycle == CYCLES - 1 else r)
-
-    final = pltpu.make_async_copy(last, resid_hbm, load_sem.at[1])
-    final.start()
-    store.wait()
-    final.wait()
+        back_all.wait_send()
 
 
 def body(forcing, start, element_class_index, class_coef):
@@ -495,36 +507,31 @@
     vmem = pltpu.VMEM
     dma = pltpu.SemaphoreType.DMA
     scratch = (
-        [vmem(full, F32), vmem((3,) + full, F32), vmem((2,) + full, F32), vmem(full, F32), vmem(full, F32)]
+        [vmem(full, F32), vmem((2,) + full, F32), vmem((2,) + full, F32), vmem(full, F32), vmem(full, F32)]
         + [vmem(brick, F32)] * 3
         + [vmem(full, F32)] * 2
         + [vmem((17, 32, 128), F32), vmem((2, 32, 128), F32)]
         + [vmem(brick, F32)] * 2
         + [vmem((2, 4, 8, 128), F32)]
         + [vmem(brick, F32)] * 3
-        + [vmem((5, 2, 32, 128), F32), vmem((5, 2, 16, 128), F32), vmem((5, 2, 8, 128), F32)]
-        + [vmem((5, 2, 16, 128), F32), vmem((5, 8, 128), F32)]
-        + [vmem((2, 32, 128), F32), vmem((2, 8, 128), F32), vmem((2, 8, 128), F32)]
-        + [vmem((8, 128), F32)] * 3
-        + [vmem((128, 256), BF16), vmem((256, 256), BF16), vmem((256, 256), BF16), vmem((128, 128), BF16)]
-        + [vmem((256, 256), BF16), vmem((32, 256), BF16), vmem((256, 256), BF16), vmem((16, 256), BF16)]
-        + [vmem((96, 256), BF16), vmem((128, 512), BF16), vmem((128, 128), F32), vmem((256, 512), F32)]
+        + [vmem((5, 112, 128), F32), vmem((5, 2, 16, 128), F32), vmem((5, 8, 128), F32)]
+        + [vmem((96, 128), F32), vmem((8, 128), F32), vmem((8, 128), F32), vmem((6, 8, 128), F32)]
+        + [vmem((1120, 256), BF16), vmem((528, 256), BF16), vmem((32, 256), BF16)]
+        + [vmem((128, 128), F32), vmem((256, 512), F32)]
         + [vmem((256, 256), BF16), vmem((64, 128), F32), vmem((128, 128), F32)]
         + [vmem((2, 32, 8, 128), BF16), vmem((2, 32, 8, 128), BF16), vmem((2, 16, 4, 16, 128), BF16)]
-        + [vmem((2, 32, 2, 8, 128), BF16), vmem((2, 8, 2, 8, 128), BF16), vmem(full, F32)]
-        + [dma((13,)), dma((2, 6)), dma((2, 6)), dma((6,)), dma((6,))]
-        + [dma((2, 32))] * 2
-        + [dma((2, 16))] * 2
-        + [dma((2, 32))] * 2
+        + [vmem((2, 32, 2, 8, 128), BF16), vmem((2, 8, 2, 8, 128), BF16)]
+        + [dma((6,)), dma((5,)), dma((5,)), dma((1,)), dma((1,))]
+        + [dma((2,))] * 6
     )
     anywhere = pl.BlockSpec(memory_space=pl.ANY)
     scalar = pl.BlockSpec(memory_space=pltpu.SMEM)
-    shape = jax.ShapeDtypeStruct(full, F32)
+    shape = pltpu.VMEM(full, F32)
     return pl.pallas_call(
         kernel,
         out_shape=(shape, shape),
-        in_specs=[anywhere, anywhere, pl.BlockSpec(memory_space=pltpu.VMEM), scalar, scalar] + [anywhere] * 11,
-        out_specs=(anywhere, anywhere),
+        in_specs=[anywhere, anywhere, pl.BlockSpec(memory_space=pltpu.VMEM), scalar, scalar] + [anywhere] * 4,
+        out_specs=(pl.BlockSpec(memory_space=pltpu.VMEM),) * 2,
         scratch_shapes=scratch,
         compiler_params=pltpu.CompilerParams(collective_id=0, has_side_effects=True),
         name="cycles",

time: 75.9 us -> 69.4 us (0.914)
  Pallas kernels: 72.6 us -> 67.2 us
  local copies, waits for them, and re-layouts: 2.42 us -> 1.41 us
    pallas_call x1, Pallas kernels: 72.6 us -> 67.2 us  [body(): pl.pallas_call(kernel, out_shape=(shape, shape), in_specs=[anywhere, anyw...]
    unnamed x4 -> x2, local copies, waits for them, and re-layouts: 2.42 us -> 1.41 us
where the time goes in v3:
time: 69.4 us; the launch traced here: 69.3 us
  Pallas kernels  67.2 us (97%)
  local copies, waits for them, and re-layouts  1.41 us (2%)
    pallas_call x1, Pallas kernels, body(): pl.pallas_call(kernel, out_shape=(shape, shape), in_specs=[anywhere, anyw...  67.2 us
    unnamed x2, local copies, waits for them, and re-layouts  1.41 us

profile of v3, /device:TPU:1, one launch (start us, length us, event | category | flops | bytes accessed | tf_op | source)
XLA Modules:
  0.0 69.3 jit_solution(13433194623094564561)
XLA Ops:
  0.6 67.2 %cycles.1 = (f32[16,32,128]{2,1,0:T(8,128)S(1)}, f32[16,32,128]{2,1,0:T(8,128)S(1)}) custom-call(f32[16,32,128]{2,1,0:T(8,128)} %forcing_hbm.1, f32[16,32,128]{2,1,0:T(8,128)} %start_hbm.1, s32[32,32]{1,0:T(8,128)} %bitcast.1, f32[3,16]{1,0:T(4,128)} %coef.1, f32[256]{0:T(256)} %constant.14.clone.eigen_y, bf16[1120,256]{1,0:T(8,128)(2,1)} %constant.10.clone.common_hbm, ...), custom_call_target="tpu_custom_call" | custom-call | tf_op jit(solution)/shard_map/cycles/pallas_call | solution.py:530
  67.8 0.7 %copy.13 = f32[16,32,128]{2,1,0:T(8,128)} copy(f32[16,32,128]{2,1,0:T(8,128)S(1)} %get-tuple-element.2) | data formatting | bytes 524288
  68.6 0.7 %copy.14 = f32[16,32,128]{2,1,0:T(8,128)} copy(f32[16,32,128]{2,1,0:T(8,128)S(1)} %get-tuple-element.3) | data formatting | bytes 524288

commit v4 on v3

--- a/solution.py
+++ b/solution.py
@@ -105,10 +105,10 @@
 
 
 def kernel(
-    forcing_hbm, start_hbm, class_ref, coef, eigen_y, common_hbm, along_hbm, ix_hbm, plane_hbm,
+    forcing_hbm, start_hbm, class_hbm, coef_hbm, eigen_hbm, common_hbm, along_hbm, ix_hbm, plane_hbm,
     out_ref, resid_ref,
     f, s, z, r, inner, kap, beta, base, diag, dinv, wx, wxb, wzl, wzh, wzb, wyl, wyh, wyb,
-    halos, zsend, ysend, khalo, kzsend, kysend, yadd,
+    class_ref, coef, eigen_y, halos, zsend, ysend, khalo, kzsend, kysend, yadd,
     common, along, ix, plane, invlam, fine, swap, wide_swap,
     va, vsend, xg, vb, vbsend,
     load_sem, halo_s, halo_r, kap_s, kap_r, z1_s, z1_r, x_s, x_r, z2_s, z2_r,
@@ -118,14 +118,12 @@
         pltpu.make_async_copy(src, dst, load_sem.at[i])
         for i, (src, dst) in enumerate(
             [
-                (start_hbm, s.at[0]), (forcing_hbm, f), (plane_hbm, plane),
+                (start_hbm, s.at[0]), (class_hbm, class_ref), (coef_hbm, coef), (eigen_hbm, eigen_y),
+                (plane_hbm, plane), (forcing_hbm, f),
                 (common_hbm, common), (along_hbm.at[iy], along), (ix_hbm.at[ib], ix),
             ]
         )
     ]
-    for load in loads:
-        load.start()
-
     def x_peer(offset):
         return lax.rem(ib // 4 + offset[0], 4) * 4 + lax.rem(lax.rem(ib, 4) + offset[1], 4)
 
@@ -139,11 +137,16 @@
         py, pz_ = plane_peer(offset)
         pl.semaphore_signal(barrier, inc=1, device_id={"by": py, "bz": pz_}, device_id_type=MESH)
 
+    for load in loads:
+        load.start()
+
     row = lax.broadcasted_iota(jnp.int32, (32, 128), 0)
     lane = lax.broadcasted_iota(jnp.int32, (32, 128), 1)
     spread_y = (lax.broadcasted_iota(jnp.int32, (32, 128), 1) // 4 == row).astype(F32).astype(BF16)
     tall = lax.broadcasted_iota(jnp.int32, (128, 32), 0) // 4
     spread_z = (tall == lax.broadcasted_iota(jnp.int32, (128, 32), 1)).astype(F32).astype(BF16)
+    loads[1].wait()
+    loads[2].wait()
     labels = class_ref[...].astype(F32).astype(BF16)
     labels = jnp.dot(labels, spread_y, preferred_element_type=F32).astype(BF16)
     labels = jnp.dot(spread_z, labels, preferred_element_type=F32)
@@ -250,7 +253,8 @@
     for index in range(1, 16):
         kbar, sbar = kbar + coef[0, index], sbar + coef[1, index]
     kbar, sbar = kbar * 0.0625, sbar * 0.0625
-    loads[2].wait()
+    loads[3].wait()
+    loads[4].wait()
     mode = iy * 64 + iz * 8
     for member in range(2):
         for pair in range(4):
@@ -361,8 +365,7 @@
             restricted(e, planes)
 
     block = lax.broadcasted_iota(jnp.int32, (8, 128), 1) // 16
-    loads[1].wait()
-    for load in loads[3:]:
+    for load in loads[5:]:
         load.wait()
     halo_wait(0)
     outer_sum(*arrived(0))
@@ -420,8 +423,6 @@
         outer_sum(*arrived(2 * cycle + 1))
         after[...] = s[cycle] + ((2.0 - DAMPING) * smooth[...] + dinv[...] * inner[...])
         pack(after, 2 * cycle + 2)
-        for copy in halo(after, 2 * cycle + 2):
-            copy.start()
         some = xg.at[cycle, pl.ds(0, 15)]
         x_all = remote(some, some, x_s.at[cycle], x_r.at[cycle], {"bx": xa})
         x_all.wait_recv()
@@ -455,6 +456,8 @@
 
         for o in PLANE:
             backward(o).start()
+        for copy in halo(after, 2 * cycle + 2):
+            copy.start()
         vb[cycle, me] = vbsend[cycle, iz]
         x_all.wait_send()
         halo_wait(2 * cycle + 2)
@@ -514,6 +517,7 @@
         + [vmem(brick, F32)] * 2
         + [vmem((2, 4, 8, 128), F32)]
         + [vmem(brick, F32)] * 3
+        + [vmem((32, 32), jnp.int32), pltpu.SMEM((3, 16), F32), pltpu.SMEM((256,), F32)]
         + [vmem((5, 112, 128), F32), vmem((5, 2, 16, 128), F32), vmem((5, 8, 128), F32)]
         + [vmem((96, 128), F32), vmem((8, 128), F32), vmem((8, 128), F32), vmem((6, 8, 128), F32)]
         + [vmem((1120, 256), BF16), vmem((528, 256), BF16), vmem((32, 256), BF16)]
@@ -521,16 +525,15 @@
         + [vmem((256, 256), BF16), vmem((64, 128), F32), vmem((128, 128), F32)]
         + [vmem((2, 32, 8, 128), BF16), vmem((2, 32, 8, 128), BF16), vmem((2, 16, 4, 16, 128), BF16)]
         + [vmem((2, 32, 2, 8, 128), BF16), vmem((2, 8, 2, 8, 128), BF16)]
-        + [dma((6,)), dma((5,)), dma((5,)), dma((1,)), dma((1,))]
+        + [dma((9,)), dma((5,)), dma((5,)), dma((1,)), dma((1,))]
         + [dma((2,))] * 6
     )
     anywhere = pl.BlockSpec(memory_space=pl.ANY)
-    scalar = pl.BlockSpec(memory_space=pltpu.SMEM)
     shape = pltpu.VMEM(full, F32)
     return pl.pallas_call(
         kernel,
         out_shape=(shape, shape),
-        in_specs=[anywhere, anywhere, pl.BlockSpec(memory_space=pltpu.VMEM), scalar, scalar] + [anywhere] * 4,
+        in_specs=[anywhere] * 9,
         out_specs=(pl.BlockSpec(memory_space=pltpu.VMEM),) * 2,
         scratch_shapes=scratch,
         compiler_params=pltpu.CompilerParams(collective_id=0, has_side_effects=True),

time: 69.4 us -> 68.2 us (0.983)
  Pallas kernels: 67.2 us -> 66 us
    pallas_call x1, Pallas kernels: 67.2 us -> 66 us  [body(): pl.pallas_call(kernel, out_shape=(shape, shape), in_specs=[anywhere] * 9,...]
where the time goes in v4:
time: 68.2 us; the launch traced here: 68 us
  Pallas kernels  66 us (97%)
  local copies, waits for them, and re-layouts  1.41 us (2%)
    pallas_call x1, Pallas kernels, body(): pl.pallas_call(kernel, out_shape=(shape, shape), in_specs=[anywhere] * 9,...  66 us
    unnamed x2, local copies, waits for them, and re-layouts  1.41 us

profile of v4, /device:TPU:1, one launch (start us, length us, event | category | flops | bytes accessed | tf_op | source)
XLA Modules:
  0.0 68.0 jit_solution(10988676386134981655)
XLA Ops:
  0.6 66.0 %cycles.1 = (f32[16,32,128]{2,1,0:T(8,128)S(1)}, f32[16,32,128]{2,1,0:T(8,128)S(1)}) custom-call(f32[16,32,128]{2,1,0:T(8,128)} %forcing_hbm.1, f32[16,32,128]{2,1,0:T(8,128)} %start_hbm.1, s32[32,32]{1,0:T(8,128)} %bitcast.1, f32[3,16]{1,0:T(4,128)} %coef_hbm.1, f32[256]{0:T(256)} %constant.14.clone.eigen_hbm, bf16[1120,256]{1,0:T(8,128)(2,1)} %constant.10.clone.common_hbm, ...), custom_call_target="tpu_custom_call" | custom-call | tf_op jit(solution)/shard_map/cycles/pallas_call | solution.py:533
  66.6 0.7 %copy.13 = f32[16,32,128]{2,1,0:T(8,128)} copy(f32[16,32,128]{2,1,0:T(8,128)S(1)} %get-tuple-element.2) | data formatting | bytes 524288
  67.3 0.7 %copy.14 = f32[16,32,128]{2,1,0:T(8,128)} copy(f32[16,32,128]{2,1,0:T(8,128)S(1)} %get-tuple-element.3) | data formatting | bytes 524288

commit v5 on v4

--- a/solution.py
+++ b/solution.py
@@ -131,13 +131,21 @@
         return lax.rem(iy + offset[0], NBY), lax.rem(iz + offset[1], NBZ)
 
     barrier = pltpu.get_barrier_semaphore()
-    for offset in OFFSETS:
-        pl.semaphore_signal(barrier, inc=1, device_id={"bx": x_peer(offset)}, device_id_type=MESH)
-    for offset in PLANE[::-1]:
-        py, pz_ = plane_peer(offset)
-        pl.semaphore_signal(barrier, inc=1, device_id={"by": py, "bz": pz_}, device_id_type=MESH)
-
-    for load in loads:
+
+    def greet(x_offsets, plane_offsets):
+        for offset in x_offsets:
+            pl.semaphore_signal(barrier, inc=1, device_id={"bx": x_peer(offset)}, device_id_type=MESH)
+        for offset in plane_offsets:
+            py, pz_ = plane_peer(offset)
+            pl.semaphore_signal(barrier, inc=1, device_id={"by": py, "bz": pz_}, device_id_type=MESH)
+
+    near_x, near_plane = [(0, 1), (0, 3), (1, 1), (3, 3)], [(0, 1), (0, 7), (1, 0), (3, 0)]
+    greet(near_x, near_plane)
+    loads[0].start()
+    loads[1].start()
+    loads[2].start()
+    greet([o for o in OFFSETS if o not in near_x], [o for o in PLANE if o not in near_plane])
+    for load in loads[3:]:
         load.start()
 
     row = lax.broadcasted_iota(jnp.int32, (32, 128), 0)

time: 68.2 us -> 67.7 us (level)
  no operation moved by 1% of the time
where the time goes in v5:
time: 67.7 us; the launch traced here: 67.5 us
  Pallas kernels  65.5 us (97%)
  local copies, waits for them, and re-layouts  1.41 us (2%)
    pallas_call x1, Pallas kernels, body(): pl.pallas_call(kernel, out_shape=(shape, shape), in_specs=[anywhere] * 9,...  65.5 us
    unnamed x2, local copies, waits for them, and re-layouts  1.41 us

profile of v5, /device:TPU:1, one launch (start us, length us, event | category | flops | bytes accessed | tf_op | source)
XLA Modules:
  0.0 67.5 jit_solution(13320234086141655140)
XLA Ops:
  0.6 65.5 %cycles.1 = (f32[16,32,128]{2,1,0:T(8,128)S(1)}, f32[16,32,128]{2,1,0:T(8,128)S(1)}) custom-call(f32[16,32,128]{2,1,0:T(8,128)} %forcing_hbm.1, f32[16,32,128]{2,1,0:T(8,128)} %start_hbm.1, s32[32,32]{1,0:T(8,128)} %bitcast.1, f32[3,16]{1,0:T(4,128)} %coef_hbm.1, f32[256]{0:T(256)} %constant.14.clone.eigen_hbm, bf16[1120,256]{1,0:T(8,128)(2,1)} %constant.10.clone.common_hbm, ...), custom_call_target="tpu_custom_call" | custom-call | tf_op jit(solution)/shard_map/cycles/pallas_call | solution.py:541
  66.1 0.7 %copy.13 = f32[16,32,128]{2,1,0:T(8,128)} copy(f32[16,32,128]{2,1,0:T(8,128)S(1)} %get-tuple-element.2) | data formatting | bytes 524288
  66.8 0.7 %copy.14 = f32[16,32,128]{2,1,0:T(8,128)} copy(f32[16,32,128]{2,1,0:T(8,128)S(1)} %get-tuple-element.3) | data formatting | bytes 524288
